TPU v7x, 128 devices: a whole 4x4x4 slice. The times are simulated.
128 devices in a mesh: dom: 16 (over y, x), sub: 8 (over z, core).
Axes of the slice: x: 4, y: 4, z: 4, core: 2. Of those that a mesh axis runs over, the one named last changes fastest.
Arguments:
- history: bfloat16 [4096, 64, 128], P(('dom', 'sub')), may hold values from -6 to 6
- send_list: int32 [128, 128, 1], P(('dom', 'sub')), may hold values from 0 to 31
- send_count: int32 [128, 128], P(('dom', 'sub')), may hold values from 0 to 1, as said below
- mixed_mass: bfloat16 [16384, 128, 128], P(('dom', 'sub')), may hold values from -0.5 to 0.5
- relay_list: int32 [128, 128, 1], P(('dom', 'sub')), may hold values from 0 to 127, as said below
- relay_target: int32 [128, 128, 1], P(('dom', 'sub')), may hold values from 0 to 63
- mass_diag: float32 [8192, 128, 128], P(('dom', 'sub')), as said below
- mass_next: float32 [8192, 128, 128], P(('dom', 'sub')), may hold values from -0.18 to 0.18
- coupling: int32 [8192], P(('dom', 'sub')), may hold values 0 or 1
- precond: float32 [8192, 128, 128], P(('dom', 'sub')), as said below
Outputs:
- solution: float32 [8192, 64, 128], P(('dom', 'sub'))
- residual: float32 [8192, 64, 128], P(('dom', 'sub'))
Inputs may be any that keep to these rules, and one draw needn't show every extreme that they name: `send_count`: live slots are the first ones. Every sender fills all 1 slots for some peer, and in every draw some receiver gets 1 live slots from every sender. For each owner e, the entries of relay_list[e] are a permutation of 0 .. 127. `mass_diag`: each block is symmetric; the assembled mass matrix is symmetric positive definite. `precond`: each block is symmetric positive definite.
All inputs are finite; a program needn't handle non-finite values. No bound on the sum of `coupling` on one device may be relied on, other than what follows from the above.
Results may differ from a plain program's by a relative error of at most 0.0003.
Values may be sent and summed in bfloat16 or wider, within the bound.
A program may use at most 128 MiB of HBM per device.

v0:
```python
import jax
import jax.numpy as jnp
from jax import lax
from jax.sharding import PartitionSpec as P

ITERS = 3


def shifted(value, axis, steps):
    count = lax.axis_size(axis)
    first, last = (max(0, -steps), min(count, count - steps))
    return lax.ppermute(value, axis, [(source, source + steps) for source in range(first, last)])


def apply_mass(field, mass_diag, mass_next, links):
    highest = lax.Precision.HIGHEST
    carried = links * jnp.einsum("gvs,gsr->gvr", field, mass_next, precision=highest)
    first_next = shifted(field[:1], ("dom", "sub"), -1)
    last_prev = shifted(carried[-1:], ("dom", "sub"), 1)
    ahead = jnp.concatenate([field[1:], first_next], axis=0)
    behind = jnp.concatenate([last_prev, carried[:-1]], axis=0)
    own = jnp.einsum("gvs,grs->gvr", field, mass_diag, precision=highest)
    onward = links * jnp.einsum("gvs,grs->gvr", ahead, mass_next, precision=highest)
    return own + onward + behind


def precondition(field, precond):
    return jnp.einsum("gvs,grs->gvr", field, precond, precision=lax.Precision.HIGHEST)


def local_inner(first, second):
    return jnp.sum(first * second, axis=(0, 2))


def squares(residual, reduced):
    return lax.psum(local_inner(residual, reduced), ("dom", "sub"))


def body(
    history,
    send_list,
    send_count,
    mixed_mass,
    relay_list,
    relay_target,
    mass_diag,
    mass_next,
    coupling,
    precond,
):
    devices = lax.axis_size(("dom", "sub"))
    slots = send_list.shape[2]
    values = history.shape[1]
    rows = history.shape[2]
    new_count = mass_diag.shape[0]
    picks = send_list[0]
    live = jnp.arange(slots, dtype=jnp.int32)[None, :] < send_count[0][:, None]
    outgoing = jnp.where(live[:, :, None, None], history[picks], jnp.zeros((), jnp.bfloat16))
    arrived = lax.all_to_all(outgoing, ("dom", "sub"), split_axis=0, concat_axis=0, tiled=True)
    mixing = mixed_mass.reshape(devices, slots, rows, rows)
    tiles = jnp.einsum("dcvs,dcsr->dcvr", arrived, mixing, preferred_element_type=jnp.float32)
    flat_tiles = tiles.reshape(devices * slots, values, rows)
    sending = flat_tiles[relay_list[0].reshape(-1)].reshape(devices, slots, values, rows)
    received = lax.all_to_all(sending, ("dom", "sub"), split_axis=0, concat_axis=0, tiled=True)
    received = received.reshape(devices * slots, values, rows)
    targets = relay_target[0].reshape(-1)
    selector = (targets[:, None] == jnp.arange(new_count, dtype=jnp.int32)[None, :]).astype(
        jnp.float32
    )
    rhs = jnp.einsum("kb,kvr->bvr", selector, received, precision=lax.Precision.HIGHEST)
    links = coupling.astype(jnp.float32)[:, None, None]
    solution = jnp.zeros_like(rhs)
    residual = rhs
    reduced = precondition(residual, precond)
    direction = reduced
    norm_now = squares(residual, reduced)
    for iteration in range(ITERS):
        image = apply_mass(direction, mass_diag, mass_next, links)
        curve = lax.psum(local_inner(direction, image), ("dom", "sub"))
        alpha = norm_now / curve
        solution = solution + alpha[None, :, None] * direction
        residual = residual - alpha[None, :, None] * image
        if iteration + 1 < ITERS:
            reduced = precondition(residual, precond)
            norm_next = squares(residual, reduced)
            direction = reduced + (norm_next / norm_now)[None, :, None] * direction
            norm_now = norm_next
    return (solution, residual)


def solution(mesh):
    placed = (
        P(("dom", "sub"), None, None),
        P(("dom", "sub"), None, None),
        P(("dom", "sub"), None),
        P(("dom", "sub"), None, None),
        P(("dom", "sub"), None, None),
        P(("dom", "sub"), None, None),
        P(("dom", "sub"), None, None),
        P(("dom", "sub"), None, None),
        P(("dom", "sub")),
        P(("dom", "sub"), None, None),
    )
    return jax.shard_map(
        body,
        mesh=mesh,
        in_specs=placed,
        out_specs=(P(("dom", "sub"), None, None), P(("dom", "sub"), None, None)),
        check_vma=False,
    )
```

profile of v0, /device:TPU:1, one launch (start us, length us, event | category | flops | bytes accessed | tf_op | source)
XLA Modules:
  0.0 611.9 jit_solution(16362210822701826097)
XLA Ops:
  4.5 11.5 %all-to-all-start = ((bf16[128,1,64,128]{3,2,1,0:T(8,128)(2,1)}), bf16[128,1,64,128]{3,2,1,0:T(8,128)(2,1)S(1)}, u32[]{:S(2)}, u32[]{:S(2)}) async-start(bf16[128,1,64,128]{3,2,1,0:T(8,128)(2,1)} %bitcast_select_fusion), calls=%async_computation | async-start | bytes 4194304 | tf_op jit(solution)/shard_map/all_to_all | solution.py:59
  16.1 30.1 %all-to-all-done = bf16[128,1,64,128]{3,2,1,0:T(8,128)(2,1)S(1)} async-done(((bf16[128,1,64,128]{3,2,1,0:T(8,128)(2,1)}), bf16[128,1,64,128]{3,2,1,0:T(8,128)(2,1)S(1)}, u32[]{:S(2)}, u32[]{:S(2)}) %all-to-all-start) | async-done | bytes 2097184 | tf_op jit(solution)/shard_map/all_to_all | solution.py:59
  46.1 5.4 fusion.7
  51.5 4.9 gather_fusion.1
  56.5 6.4 %all-to-all-start.1 = ((f32[128,1,64,128]{3,2,1,0:T(8,128)}), f32[128,1,64,128]{3,2,1,0:T(8,128)}, u32[]{:S(2)}, u32[]{:S(2)}) async-start(f32[128,1,64,128]{3,2,1,0:T(8,128)} %bitcast.43), calls=%async_computation.1 | async-start | bytes 8388608 | tf_op jit(solution)/shard_map/all_to_all | solution.py:64
  62.9 52.2 %all-to-all-done.1 = f32[128,1,64,128]{3,2,1,0:T(8,128)} async-done(((f32[128,1,64,128]{3,2,1,0:T(8,128)}), f32[128,1,64,128]{3,2,1,0:T(8,128)}, u32[]{:S(2)}, u32[]{:S(2)}) %all-to-all-start.1) | async-done | bytes 4194336 | tf_op jit(solution)/shard_map/all_to_all | solution.py:64
  115.1 6.2 %fusion = f32[64,64,128]{2,0,1:T(8,128)S(1)} fusion(f32[128,1,64,128]{3,2,1,0:T(8,128)} %all-to-all-done.1, s32[128]{0:T(128)S(1)} %bitcast.47), kind=kOutput, calls=%fused_computation.2 | convolution fusion | flops 805314560 | bytes 6291968 | tf_op jit(solution)/shard_map/kb,kvr->bvr/dot_general | solution.py:70
  121.3 8.4 %fusion.17 = f32[64,64,128]{2,1,0:T(8,128)S(1)} fusion(f32[64,128,128]{2,1,0:T(8,128)S(1)} %copy-done.7, f32[64,64,128]{2,0,1:T(8,128)S(1)} %fusion), kind=kOutput, calls=%fused_computation.34 | convolution fusion | flops 805306368 | bytes 8388608 | tf_op jit(solution)/shard_map/gvs,grs->gvr/dot_general | solution.py:28
  129.8 3.7 collective-permute-start
  133.5 3.9 fusion.34
  141.0 8.2 %fusion.33 = f32[64,64,128]{2,1,0:T(8,128)S(1)} fusion(f32[64,64,128]{2,1,0:T(8,128)S(1)} %fusion.17, f32[64,128,128]{2,1,0:T(8,128)S(1)} %copy-done.10), kind=kOutput, calls=%fused_computation.67 | convolution fusion | flops 805306368 | bytes 8388608 | tf_op jit(solution)/shard_map/gvs,grs->gvr/dot_general | solution.py:22
  149.3 8.2 %fusion.3 = f32[64,64,128]{2,1,0:T(8,128)S(1)} fusion(f32[64,128,128]{2,1,0:T(8,128)S(1)} %copy-done.2, f32[1,64,128]{2,1,0:T(8,128)S(1)} %collective-permute-done, f32[63,64,128]{2,1,0:T(8,128)S(1)} %slice.52), kind=kOutput, calls=%fused_computation.5 | convolution fusion | flops 805830656 | bytes 8388608 | tf_op jit(solution)/shard_map/gvs,grs->gvr/dot_general | solution.py:23
  157.6 8.0 %multiply_reduce_fusion.4 = (f32[64]{0:T(128)S(1)}, f32[64]{0:T(128)S(1)}, f32[64,64,128]{2,0,1:T(8,128)}) fusion(f32[64,64,128]{2,1,0:T(8,128)S(1)} %fusion.17, f32[64,64,128]{2,0,1:T(8,128)S(1)} %fusion, f32[63,64,128]{2,0,1:T(8,128)S(1)} %bitcast.44, f32[1,64,128]{2,0,1:T(1,128)S(1)} %collective-permute-done.1, f32[64,64,128]{2,1,0:T(8,128)S(1)} %fusion.3, ...), kind=kLoop, calls=%fused_computation.46 | loop fusion | flops 4194176 | bytes 12583680 | tf_op jit(solution)/shard_map/reduce_sum | solution.py:32
  165.6 66.2 %all-reduce = (f32[64]{0:T(128)S(1)}, f32[64]{0:T(128)S(1)}) all-reduce(f32[64]{0:T(128)S(1)} %get-tuple-element.7, f32[64]{0:T(128)S(1)} %get-tuple-element.6), channel_id=1, replica_groups=mesh['dom'=16,'sub'=8] {'dom','sub'}, use_global_device_ids=true, to_apply=%region_1.2 | all-reduce | flops 128 | bytes 1024 | tf_op jit(solution)/shard_map/psum | solution.py:36
  234.6 8.3 %fusion.15 = f32[64,64,128]{2,1,0:T(8,128)S(1)} fusion(f32[64,128,128]{2,1,0:T(8,128)S(1)} %copy-done.8, f32[64,64,128]{2,0,1:T(8,128)S(1)} %multiply_subtract_fusion.2), kind=kOutput, calls=%fused_computation.29 | convolution fusion | flops 805306368 | bytes 8388608 | tf_op jit(solution)/shard_map/gvs,grs->gvr/dot_general | solution.py:28
  246.4 64.5 %psum.44 = f32[64]{0:T(128)S(1)} all-reduce(f32[64]{0:T(128)S(1)} %multiply_reduce_fusion.3), channel_id=1, replica_groups=mesh['dom'=16,'sub'=8] {'dom','sub'}, use_global_device_ids=true, to_apply=%region_5.6 | all-reduce | flops 64 | bytes 512 | tf_op jit(solution)/shard_map/psum | solution.py:36
  310.9 4.7 multiply_add_fusion.2
  315.7 4.9 fusion.23
  320.7 8.5 %fusion.25 = f32[64,64,128]{2,1,0:T(8,128)S(1)} fusion(f32[64,128,128]{2,1,0:T(8,128)S(1)} %copy-done.11, f32[64,64,128]{2,0,1:T(8,128)S(1)} %multiply_add_fusion.2), kind=kOutput, calls=%fused_computation.54 | convolution fusion | flops 805306368 | bytes 8388608 | tf_op jit(solution)/shard_map/gvs,grs->gvr/dot_general | solution.py:22
  333.5 2.8 collective-permute-start.3
  336.6 8.5 %fusion.13 = f32[64,64,128]{2,1,0:T(8,128)S(1)} fusion(f32[64,128,128]{2,1,0:T(8,128)S(1)} %copy-done.3, f32[64,64,128]{2,0,1:T(8,128)S(1)} %pad_maximum_fusion), kind=kOutput, calls=%fused_computation.27 | convolution fusion | flops 805306368 | bytes 8388608 | tf_op jit(solution)/shard_map/gvs,grs->gvr/dot_general | solution.py:23
  345.0 5.2 multiply_reduce_fusion.2
  350.3 66.7 %psum.45 = f32[64]{0:T(128)S(1)} all-reduce(f32[64]{0:T(128)S(1)} %get-tuple-element.12), channel_id=1, replica_groups=mesh['dom'=16,'sub'=8] {'dom','sub'}, use_global_device_ids=true, to_apply=%region_7.8 | all-reduce | flops 64 | bytes 512 | tf_op jit(solution)/shard_map/psum | solution.py:79
  420.4 8.3 %fusion.11 = f32[64,64,128]{2,1,0:T(8,128)S(1)} fusion(f32[64,128,128]{2,1,0:T(8,128)S(1)} %copy-done.9, f32[64,64,128]{2,0,1:T(8,128)S(1)} %multiply_subtract_fusion.1), kind=kOutput, calls=%fused_computation.22 | convolution fusion | flops 805306368 | bytes 8388608 | tf_op jit(solution)/shard_map/gvs,grs->gvr/dot_general | solution.py:28
  432.2 64.3 %psum.46 = f32[64]{0:T(128)S(1)} all-reduce(f32[64]{0:T(128)S(1)} %multiply_reduce_fusion.1), channel_id=1, replica_groups=mesh['dom'=16,'sub'=8] {'dom','sub'}, use_global_device_ids=true, to_apply=%region_9.10 | all-reduce | flops 64 | bytes 512 | tf_op jit(solution)/shard_map/psum | solution.py:36
  496.5 3.1 multiply_add_fusion.1
  499.7 5.1 fusion.19
  504.8 8.6 %fusion.21 = f32[64,64,128]{2,1,0:T(8,128)S(1)} fusion(f32[64,128,128]{2,1,0:T(8,128)S(1)} %copy-done.12, f32[64,64,128]{2,0,1:T(8,128)S(1)} %multiply_add_fusion.1), kind=kOutput, calls=%fused_computation.50 | convolution fusion | flops 805306368 | bytes 8388608 | tf_op jit(solution)/shard_map/gvs,grs->gvr/dot_general | solution.py:22
  520.8 8.5 %fusion.9 = f32[64,64,128]{2,1,0:T(8,128)S(1)} fusion(f32[64,128,128]{2,1,0:T(8,128)S(1)} %copy-done.4, f32[64,64,128]{2,0,1:T(8,128)S(1)} %pad_maximum_fusion.1), kind=kOutput, calls=%fused_computation.20 | convolution fusion | flops 805306368 | bytes 8388608 | tf_op jit(solution)/shard_map/gvs,grs->gvr/dot_general | solution.py:23
  529.3 5.1 multiply_reduce_fusion
  534.4 66.6 %psum.47 = f32[64]{0:T(128)S(1)} all-reduce(f32[64]{0:T(128)S(1)} %get-tuple-element.10), channel_id=1, replica_groups=mesh['dom'=16,'sub'=8] {'dom','sub'}, use_global_device_ids=true, to_apply=%region_11.12 | all-reduce | flops 64 | bytes 512 | tf_op jit(solution)/shard_map/psum | solution.py:79
  601.0 5.6 multiply_subtract_fusion
  (83 shorter events, 37.6 us)
Async XLA Ops:
  0.6 1.4 copy-start
  4.5 11.5 %copy-start.18 = (s32[1,128,1]{1,2,0:T(1,128)S(1)}, s32[1,128,1]{1,2,0:T(1,128)}, u32[]{:S(2)}) copy-start(s32[1,128,1]{1,2,0:T(1,128)} %param.14) | copy-start | bytes 1540
  4.5 41.6 %all-to-all-start = ((bf16[128,1,64,128]{3,2,1,0:T(8,128)(2,1)}), bf16[128,1,64,128]{3,2,1,0:T(8,128)(2,1)S(1)}, u32[]{:S(2)}, u32[]{:S(2)}) async-start(bf16[128,1,64,128]{3,2,1,0:T(8,128)(2,1)} %bitcast_select_fusion), calls=%async_computation | async-start | bytes 4194304 | tf_op jit(solution)/shard_map/all_to_all | solution.py:59
  56.5 6.4 %copy-start.19 = (s32[64]{0:T(128)S(1)}, s32[64]{0:T(128)}, u32[]{:S(2)}) copy-start(s32[64]{0:T(128)} %param.18) | copy-start | bytes 772
  56.5 58.7 %copy-start.17 = (s32[1,128,1]{1,2,0:T(1,128)S(1)}, s32[1,128,1]{1,2,0:T(1,128)}, u32[]{:S(2)}) copy-start(s32[1,128,1]{1,2,0:T(1,128)} %param.15) | copy-start | bytes 1540
  56.5 58.6 %all-to-all-start.1 = ((f32[128,1,64,128]{3,2,1,0:T(8,128)}), f32[128,1,64,128]{3,2,1,0:T(8,128)}, u32[]{:S(2)}, u32[]{:S(2)}) async-start(f32[128,1,64,128]{3,2,1,0:T(8,128)} %bitcast.43), calls=%async_computation.1 | async-start | bytes 8388608 | tf_op jit(solution)/shard_map/all_to_all | solution.py:64
  115.1 6.2 %copy-start.7 = (f32[64,128,128]{2,1,0:T(8,128)S(1)}, f32[64,128,128]{2,1,0:T(8,128)}, u32[]{:S(2)}) copy-start(f32[64,128,128]{2,1,0:T(8,128)} %param.19) | copy-start | bytes 12582916
  121.3 12.2 %copy-start.2 = (f32[64,128,128]{2,1,0:T(8,128)S(1)}, f32[64,128,128]{2,1,0:T(8,128)}, u32[]{:S(2)}) copy-start(f32[64,128,128]{2,1,0:T(8,128)} %param.17) | copy-start | bytes 12582916
  129.7 27.8 %copy-start.5 = (f32[64,64,128]{2,1,0:T(8,128)}, f32[64,64,128]{2,1,0:T(8,128)S(1)}, u32[]{:S(2)}) copy-start(f32[64,64,128]{2,1,0:T(8,128)S(1)} %fusion.17) | copy-start | bytes 6291460
  129.8 19.6 %collective-permute-start = (f32[1,64,128]{2,1,0:T(8,128)S(1)}, f32[1,64,128]{2,1,0:T(8,128)S(1)}, u32[]{:S(2)}, u32[]{:S(2)}) collective-permute-start(f32[1,64,128]{2,1,0:T(8,128)S(1)} %slice.53), channel_id=1, source_target_pairs={{1,0},{2,1},{3,2},{4,3},{5,4},{6,5},{7,6},{8,7},{9,8},{10,9},{11,1... | collective-permute-start | bytes 98312 | tf_op jit(solution)/shard_map/ppermute | solution.py:12
  137.4 3.5 copy-start.10
  138.7 18.9 %collective-permute-start.1 = (f32[1,64,128]{2,0,1:T(1,128)S(1)}, f32[1,64,128]{2,0,1:T(1,128)S(1)}, u32[]{:S(2)}, u32[]{:S(2)}) collective-permute-start(f32[1,64,128]{2,0,1:T(1,128)S(1)} %slice.54), channel_id=1, source_target_pairs={{0,1},{1,2},{2,3},{3,4},{4,5},{5,6},{6,7},{7,8},{8,9},{9,10},{10,1... | collective-permute-start | bytes 98312 | tf_op jit(solution)/shard_map/ppermute | solution.py:12
  231.8 2.8 copy-start.8
  234.6 8.4 %copy-start.13 = (f32[64,64,128]{2,0,1:T(8,128)}, f32[64,64,128]{2,0,1:T(8,128)S(1)}, u32[]{:S(2)}) copy-start(f32[64,64,128]{2,0,1:T(8,128)S(1)} %multiply_subtract_fusion.2) | copy-start | bytes 6291460
  243.0 1.3 copy-start.15
  310.9 4.8 copy-start.3
  315.7 4.9 copy-start.11
  329.2 7.1 %collective-permute-start.2 = (f32[1,64,128]{2,0,1:T(1,128)S(1)}, f32[1,64,128]{2,0,1:T(1,128)S(1)}, u32[]{:S(2)}, u32[]{:S(2)}) collective-permute-start(f32[1,64,128]{2,0,1:T(1,128)S(1)} %slice.57), channel_id=1, source_target_pairs={{1,0},{2,1},{3,2},{4,3},{5,4},{6,5},{7,6},{8,7},{9,8},{10,9},{11,1... | collective-permute-start | bytes 98312 | tf_op jit(solution)/shard_map/ppermute | solution.py:12
  333.5 11.5 %collective-permute-start.3 = (f32[1,64,128]{2,0,1:T(1,128)S(1)}, f32[1,64,128]{2,0,1:T(1,128)S(1)}, u32[]{:S(2)}, u32[]{:S(2)}) collective-permute-start(f32[1,64,128]{2,0,1:T(1,128)S(1)} %slice.58), channel_id=1, source_target_pairs={{0,1},{1,2},{2,3},{3,4},{4,5},{5,6},{6,7},{7,8},{8,9},{9,10},{10,1... | collective-permute-start | bytes 98312 | tf_op jit(solution)/shard_map/ppermute | solution.py:12
  417.0 3.5 copy-start.9
  420.4 8.4 %copy-start.14 = (f32[64,64,128]{2,0,1:T(8,128)}, f32[64,64,128]{2,0,1:T(8,128)S(1)}, u32[]{:S(2)}) copy-start(f32[64,64,128]{2,0,1:T(8,128)S(1)} %multiply_subtract_fusion.1) | copy-start | bytes 6291460
  428.8 1.3 copy-start.16
  496.5 3.1 copy-start.4
  499.6 29.7 %copy-start.6 = (f32[64,64,128]{2,0,1:T(8,128)}, f32[64,64,128]{2,0,1:T(8,128)S(1)}, u32[]{:S(2)}) copy-start(f32[64,64,128]{2,0,1:T(8,128)S(1)} %multiply_add_fusion.1) | copy-start | bytes 6291460
  499.7 5.1 copy-start.12
  513.4 7.1 %collective-permute-start.4 = (f32[1,64,128]{2,0,1:T(1,128)S(1)}, f32[1,64,128]{2,0,1:T(1,128)S(1)}, u32[]{:S(2)}, u32[]{:S(2)}) collective-permute-start(f32[1,64,128]{2,0,1:T(1,128)S(1)} %slice.61), channel_id=1, source_target_pairs={{1,0},{2,1},{3,2},{4,3},{5,4},{6,5},{7,6},{8,7},{9,8},{10,9},{11,1... | collective-permute-start | bytes 98312 | tf_op jit(solution)/shard_map/ppermute | solution.py:12
  517.7 11.6 %collective-permute-start.5 = (f32[1,64,128]{2,0,1:T(1,128)S(1)}, f32[1,64,128]{2,0,1:T(1,128)S(1)}, u32[]{:S(2)}, u32[]{:S(2)}) collective-permute-start(f32[1,64,128]{2,0,1:T(1,128)S(1)} %slice.62), channel_id=1, source_target_pairs={{0,1},{1,2},{2,3},{3,4},{4,5},{5,6},{6,7},{7,8},{8,9},{9,10},{10,1... | collective-permute-start | bytes 98312 | tf_op jit(solution)/shard_map/ppermute | solution.py:12
  609.1 2.5 copy-start.1
where the time goes:
time: 616 us; the launch traced here: 612 us
  blocking collectives  328 us (53%)
  matrix products  101 us (16%)
  waiting for transfers between devices  82.3 us (13%)
  other arithmetic  47.6 us (8%)
  starting transfers between devices  35 us (6%)
  local copies, waits for them, and re-layouts  16.2 us (3%)
    psum x3, blocking collectives, squares(): return lax.psum(local_inner(residual, reduced), ('dom', 'sub'))  195 us
    psum x2, blocking collectives, body(): curve = lax.psum(local_inner(direction, image), ('dom', 'sub'))  133 us
    all_to_all x1, waiting for transfers between devices, body(): lax.all_to_all(sending, ('dom', 'sub'), split_axis=0, concat_axis=0, tile...  52.2 us
    all_to_all x1, waiting for transfers between devices, body(): lax.all_to_all(outgoing, ('dom', 'sub'), split_axis=0, concat_axis=0, til...  30.1 us
    dot_general x3, matrix products, apply_mass(): own = jnp.einsum('gvs,grs->gvr', field, mass_diag, precision=highest)  25.3 us
    dot_general x3, matrix products, apply_mass(): jnp.einsum('gvs,grs->gvr', ahead, mass_next, precision=highest)  25.2 us
    dot_general x3, matrix products, precondition(): jnp.einsum('gvs,grs->gvr', field, precond, precision=lax.Precision.HIGHEST)  25.1 us
    reduce_sum x5, other arithmetic, local_inner(): return jnp.sum(first * second, axis=(0, 2))  22.5 us
  transfers between devices with their start and end apart: 8, of which 2 were waited for; matrix products, arithmetic and copies ran while one was open for 7% of the time, Pallas kernels for 0%

commit v1 on v0

v1 whole, which is shorter than its diff:
```python
import jax
import jax.numpy as jnp
from jax import lax
from jax.experimental import pallas as pl
from jax.experimental.pallas import tpu as pltpu
from jax.sharding import PartitionSpec as P

MESH = pl.DeviceIdType.MESH
F32 = jnp.float32
BF16 = jnp.bfloat16
STEPS = 3
CHUNK = 4


def split(value):
    high = value.astype(BF16)
    low = (value - high.astype(F32)).astype(BF16)
    return high, low


def stacked(value):
    return jnp.concatenate(split(value), axis=0)


def product(left, weights, half):
    full = jnp.dot(left, weights, preferred_element_type=F32)
    top = full[:half] + full[half:]
    width = top.shape[1] // 2
    return top[:, :width] + top[:, width:]


def solve_kernel(
    shape,
    order_ref,
    same_ref,
    last_ref,
    have_ref,
    links_ref,
    tiles_hbm,
    diag_hbm,
    next_hbm,
    prec_hbm,
    x_hbm,
    res_hbm,
    tiles,
    stage,
    wa,
    wp,
    diag_a,
    diag_p,
    res,
    red,
    xs,
    halo,
    acc,
    trace,
    inv,
    red_src,
    red_dom,
    red_sub,
    tile_sem,
    stage_sem,
    halo_send,
    halo_recv,
    link_send,
    link_recv,
    dom_send,
    dom_recv,
    sub_send,
    sub_recv,
    out_sem,
):
    doms, subs, count, values, rows, slots = shape
    devices = doms * subs
    me_dom, me_sub = lax.axis_index("dom"), lax.axis_index("sub")
    me = me_dom * subs + me_sub
    after = lax.rem(me + 1, devices)
    before = lax.rem(me + devices - 1, devices)
    after_id = (after // subs, lax.rem(after, subs))
    before_id = (before // subs, lax.rem(before, subs))

    load_tiles = pltpu.make_async_copy(tiles_hbm, tiles, tile_sem)
    load_tiles.start()

    barrier = pltpu.get_barrier_semaphore()
    pl.semaphore_signal(barrier, inc=1, device_id=after_id, device_id_type=MESH)
    pl.semaphore_signal(barrier, inc=1, device_id=before_id, device_id_type=MESH)

    @pl.loop(1, doms)
    def _(j):
        pl.semaphore_signal(
            barrier, inc=1, device_id=(lax.rem(me_dom + j, doms), me_sub), device_id_type=MESH
        )

    @pl.loop(1, subs)
    def _(j):
        pl.semaphore_signal(
            barrier, inc=1, device_id=(me_dom, lax.rem(me_sub + j, subs)), device_id_type=MESH
        )

    sources = (diag_hbm, next_hbm, prec_hbm)

    def stage_copy(chunk, which):
        slot = lax.rem(chunk, 2)
        return pltpu.make_async_copy(
            sources[which].at[pl.ds(chunk * CHUNK, CHUNK)],
            stage.at[slot, which],
            stage_sem.at[slot, which],
        )

    for which in range(3):
        stage_copy(0, which).start()
    trace[...] = jnp.zeros_like(trace)
    row = lax.broadcasted_iota(jnp.int32, (rows, rows), 0)
    col = lax.broadcasted_iota(jnp.int32, (rows, rows), 1)
    eye = row == col
    chunks = count // CHUNK

    @pl.loop(0, chunks)
    def _(chunk):
        @pl.when(chunk + 1 < chunks)
        def _():
            for which in range(3):
                stage_copy(chunk + 1, which).start()

        for which in range(3):
            stage_copy(chunk, which).wait()
        slot = lax.rem(chunk, 2)

        @pl.loop(0, CHUNK)
        def _(i):
            g = chunk * CHUNK + i
            here = stage[slot, 0, i]
            onto = stage[slot, 1, i]
            prec = stage[slot, 2, i]
            trace[...] += jnp.sum((here * prec).reshape(rows // 8, 8, rows), axis=0)
            diag_a[g] = jnp.sum(jnp.where(eye, here, 0.0), axis=0, keepdims=True)
            diag_p[g] = jnp.sum(jnp.where(eye, prec, 0.0), axis=0, keepdims=True)
            high, low = split(jnp.where(eye, 0.0, here))
            wa[g, 0:rows, 0:rows] = high
            wa[g, 0:rows, rows : 2 * rows] = low
            wrap = jnp.logical_and(g == count - 1, me == devices - 1)
            link = jnp.where(wrap, 0.0, links_ref[g].astype(F32))
            onto = onto * link
            high, low = split(onto)
            wa[g + 1, 2 * rows : 3 * rows, 0:rows] = high
            wa[g + 1, 2 * rows : 3 * rows, rows : 2 * rows] = low
            high, low = split(onto.T)
            wa[g, rows : 2 * rows, 0:rows] = high
            wa[g, rows : 2 * rows, rows : 2 * rows] = low
            high, low = split(jnp.where(eye, 0.0, prec))
            wp[g, :, 0:rows] = high
            wp[g, :, rows : 2 * rows] = low

    pl.semaphore_wait(barrier, 2 + doms - 1 + subs - 1)

    def reduce_over(phase, value):
        def dom_copy(peer, slot):
            return pltpu.make_async_remote_copy(
                src_ref=red_src.at[phase, 0],
                dst_ref=red_dom.at[phase, slot],
                send_sem=dom_send.at[phase, peer],
                recv_sem=dom_recv.at[phase, slot],
                device_id=(peer, me_sub),
                device_id_type=MESH,
            )

        def sub_copy(peer, slot):
            return pltpu.make_async_remote_copy(
                src_ref=red_src.at[phase, 1],
                dst_ref=red_sub.at[phase, slot],
                send_sem=sub_send.at[phase, peer],
                recv_sem=sub_recv.at[phase, slot],
                device_id=(me_dom, peer),
                device_id_type=MESH,
            )

        red_src[phase, 0] = value
        red_dom[phase, me_dom] = value

        @pl.loop(1, doms)
        def _(j):
            dom_copy(lax.rem(me_dom + j, doms), me_dom).start()

        @pl.loop(1, doms)
        def _(j):
            other = lax.rem(me_dom + j, doms)
            dom_copy(other, other).wait_recv()

        total = red_dom[phase, 0]
        for j in range(1, doms):
            total = total + red_dom[phase, j]
        red_src[phase, 1] = total
        red_sub[phase, me_sub] = total

        @pl.loop(1, subs)
        def _(j):
            sub_copy(lax.rem(me_sub + j, subs), me_sub).start()

        @pl.loop(1, subs)
        def _(j):
            other = lax.rem(me_sub + j, subs)
            sub_copy(other, other).wait_recv()

        total = red_sub[phase, 0]
        for j in range(1, subs):
            total = total + red_sub[phase, j]

        @pl.loop(1, doms)
        def _(j):
            dom_copy(lax.rem(me_dom + j, doms), me_dom).wait_send()

        @pl.loop(1, subs)
        def _(j):
            sub_copy(lax.rem(me_sub + j, subs), me_sub).wait_send()

        return total

    link_copy = pltpu.make_async_remote_copy(
        src_ref=wa.at[count, pl.ds(2 * rows, rows)],
        dst_ref=wa.at[0, pl.ds(2 * rows, rows)],
        send_sem=link_send,
        recv_sem=link_recv,
        device_id=after_id,
        device_id_type=MESH,
    )
    link_copy.start()
    theta = reduce_over(0, trace[...])
    theta = jnp.sum(jnp.sum(theta, axis=0, keepdims=True), axis=1, keepdims=True)
    inv[...] = jnp.broadcast_to((1.0 * devices * count * rows) / theta, inv.shape)

    load_tiles.wait()
    acc[0] = jnp.zeros_like(acc[0])

    def add_tile(j, running):
        running = running * same_ref[j] + tiles[order_ref[j]]
        red[j] = running
        return running

    lax.fori_loop(0, slots, add_tile, jnp.zeros((values, rows), F32))

    @pl.loop(0, count)
    def _(g):
        res[0, g] = red[last_ref[g]] * have_ref[g]

    def precondition(g, k, value):
        out = product(stacked(value), wp[g], values) + value * diag_p[g]
        red[k * count + g] = out
        xs[k % 2, g + 1] = stacked(out)

    def apply_block(g, k, left, right):
        here = xs[k % 2, g + 1]
        image = product(jnp.concatenate([here, right, left], axis=1), wa[g], values)
        field = red[k * count + g]
        image = image + field * diag_a[g]
        now = res[k, g]
        later = now - image * inv[0:1]
        res[k + 1, g] = later
        step = now - later
        if k == 0:
            acc[0] += field * step
        if k == 1:
            acc[1] += field * (res[0, g] - now)
            acc[2] += field * step
        if k == 2:
            acc[3] += field * (res[1, g] - now)
            acc[4] += field * step
            acc[5] += red[g] * later
            acc[6] += red[count + g] * later
            acc[7] += field * later
        if k + 1 < STEPS:
            precondition(g, k + 1, later)

    def inner(g, k):
        apply_block(g, k, xs[k % 2, g], xs[k % 2, g + 2])

    def halo_copy(k, side):
        return pltpu.make_async_remote_copy(
            src_ref=xs.at[k % 2, count if side == 0 else 1],
            dst_ref=halo.at[k, side],
            send_sem=halo_send.at[k, side],
            recv_sem=halo_recv.at[k, side],
            device_id=after_id if side == 0 else before_id,
            device_id_type=MESH,
        )

    middle = count // 2
    acc[...] = jnp.zeros_like(acc)
    precondition(0, 0, res[0, 0])
    precondition(count - 1, 0, res[0, count - 1])

    @pl.loop(1, 9)
    def _(g):
        precondition(g, 0, res[0, g])

    halo_copy(0, 0).start()
    halo_copy(0, 1).start()

    @pl.loop(9, count - 1)
    def _(g):
        precondition(g, 0, res[0, g])

    link_copy.wait()
    for k in range(STEPS):

        @pl.loop(1, middle)
        def _(g):
            inner(g, k)

        halo_copy(k, 0).wait()
        halo_copy(k, 1).wait()
        apply_block(0, k, halo[k, 0], xs[k % 2, 2])
        apply_block(count - 1, k, xs[k % 2, count - 1], halo[k, 1])

        @pl.loop(middle, middle + 4)
        def _(g):
            inner(g, k)

        if k + 1 < STEPS:
            halo_copy(k + 1, 0).start()
            halo_copy(k + 1, 1).start()

        @pl.loop(middle + 4, count - 1)
        def _(g):
            inner(g, k)

    lane = lax.broadcasted_iota(jnp.int32, (values, rows), 1)
    packed = jnp.zeros((values, rows), F32)
    for j in range(8):
        packed = packed + jnp.where(lane == j, jnp.sum(acc[j], axis=1, keepdims=True), 0.0)
    packed = jnp.concatenate([packed, jnp.zeros((rows - values, rows), F32)], axis=0)
    total = reduce_over(1, packed.T[0:8])

    def over(top, bottom):
        usable = bottom != 0.0
        return jnp.where(usable, top / jnp.where(usable, bottom, 1.0), 0.0)

    g00, g10, g11, g21, g22 = (total[j : j + 1] for j in range(5))
    h0, h1, h2 = (-total[j : j + 1] for j in range(5, 8))
    l1, l2 = over(g10, g00), over(g11, g00)
    d1 = g11 - l1 * g10
    mix = g21 - l2 * g10
    l3 = over(mix, d1)
    d2 = g22 - l2 * g11 - l3 * mix
    y1 = h1 - l1 * h0
    y2 = h2 - l2 * h0 - l3 * y1
    e2 = over(y2, d2)
    e1 = over(y1, d1) - l3 * e2
    e0 = over(h0, g00) - l1 * e1 - l2 * e2
    weights = jnp.concatenate([e0, e1, e2, jnp.zeros((rows - 3, rows), F32)], axis=0).T
    e0 = jnp.broadcast_to(weights[0:values, 0:1], (values, rows))
    e1 = jnp.broadcast_to(weights[0:values, 1:2], (values, rows))
    e2 = jnp.broadcast_to(weights[0:values, 2:3], (values, rows))
    scale = inv[0:1]
    x0, x1, x2 = (1.0 - e0) * scale, (1.0 - e1) * scale, (1.0 - e2) * scale
    r1, r2, r3 = e1 - e0, e2 - e1, 1.0 - e2

    @pl.loop(0, count)
    def _(g):
        u0, u1, u2 = red[g], red[count + g], red[2 * count + g]
        red[g] = x0 * u0 + x1 * u1 + x2 * u2
        res[0, g] = e0 * res[0, g] + r1 * res[1, g] + r2 * res[2, g] + r3 * res[3, g]

    put_x = pltpu.make_async_copy(red.at[pl.ds(0, count)], x_hbm, out_sem.at[0])
    put_r = pltpu.make_async_copy(res.at[0], res_hbm, out_sem.at[1])
    put_x.start()
    put_r.start()
    put_x.wait()
    put_r.wait()


def mass_solve(order, same, last, have, links, tiles, mass_diag, mass_next, precond):
    doms, subs = lax.axis_size("dom"), lax.axis_size("sub")
    slots, values, rows = tiles.shape
    count = mass_diag.shape[0]
    shape = (doms, subs, count, values, rows, slots)

    def kernel(*refs):
        solve_kernel(shape, *refs)

    smem = pl.BlockSpec(memory_space=pltpu.SMEM)
    hbm = pl.BlockSpec(memory_space=pl.ANY)
    field = jax.ShapeDtypeStruct((count, values, rows), F32)
    dma = pltpu.SemaphoreType.DMA
    return pl.pallas_call(
        kernel,
        out_shape=(field, field),
        in_specs=[smem] * 5 + [hbm] * 4,
        out_specs=(hbm, hbm),
        scratch_shapes=[
            pltpu.VMEM((slots, values, rows), F32),
            pltpu.VMEM((2, 3, CHUNK, rows, rows), F32),
            pltpu.VMEM((count + 1, 3 * rows, 2 * rows), BF16),
            pltpu.VMEM((count, rows, 2 * rows), BF16),
            pltpu.VMEM((count, 1, rows), F32),
            pltpu.VMEM((count, 1, rows), F32),
            pltpu.VMEM((STEPS + 1, count, values, rows), F32),
            pltpu.VMEM((STEPS * count, values, rows), F32),
            pltpu.VMEM((2, count + 2, 2 * values, rows), BF16),
            pltpu.VMEM((STEPS, 2, 2 * values, rows), BF16),
            pltpu.VMEM((8, values, rows), F32),
            pltpu.VMEM((8, rows), F32),
            pltpu.VMEM((8, rows), F32),
            pltpu.VMEM((2, 2, 8, rows), F32),
            pltpu.VMEM((2, doms, 8, rows), F32),
            pltpu.VMEM((2, subs, 8, rows), F32),
            dma,
            dma((2, 3)),
            dma((STEPS, 2)),
            dma((STEPS, 2)),
            dma,
            dma,
            dma((2, doms)),
            dma((2, doms)),
            dma((2, subs)),
            dma((2, subs)),
            dma((2,)),
        ],
        compiler_params=pltpu.CompilerParams(
            collective_id=0, has_side_effects=True, vmem_limit_bytes=60 * 1024 * 1024
        ),
    )(order, same, last, have, links, tiles, mass_diag, mass_next, precond)


def target_order(targets, count):
    slots = targets.shape[0]
    spot = jnp.arange(slots, dtype=jnp.int32)
    key = targets * slots + spot
    rank = jnp.sum((key[None, :] < key[:, None]).astype(jnp.int32), axis=1)
    at = rank[None, :] == spot[:, None]
    order = jnp.sum(jnp.where(at, spot[None, :], 0), axis=1)
    ordered = jnp.sum(jnp.where(at, targets[None, :], 0), axis=1)
    same = jnp.concatenate([jnp.zeros((1,), F32), (ordered[1:] == ordered[:-1]).astype(F32)])
    block = jnp.arange(count, dtype=jnp.int32)
    upto = jnp.sum((targets[None, :] <= block[:, None]).astype(jnp.int32), axis=1)
    have = jnp.any(targets[None, :] == block[:, None], axis=1).astype(F32)
    return order, same, jnp.maximum(upto - 1, 0), have


def body(
    history,
    send_list,
    send_count,
    mixed_mass,
    relay_list,
    relay_target,
    mass_diag,
    mass_next,
    coupling,
    precond,
):
    devices = lax.axis_size(("dom", "sub"))
    slots = send_list.shape[2]
    values = history.shape[1]
    rows = history.shape[2]
    new_count = mass_diag.shape[0]
    picks = send_list[0]
    live = jnp.arange(slots, dtype=jnp.int32)[None, :] < send_count[0][:, None]
    outgoing = jnp.where(live[:, :, None, None], history[picks], jnp.zeros((), BF16))
    arrived = lax.all_to_all(outgoing, ("dom", "sub"), split_axis=0, concat_axis=0, tiled=True)
    mixing = mixed_mass.reshape(devices, slots, rows, rows)
    tiles = jnp.einsum("dcvs,dcsr->dcvr", arrived, mixing, preferred_element_type=F32)
    flat_tiles = tiles.reshape(devices * slots, values, rows)
    sending = flat_tiles[relay_list[0].reshape(-1)].reshape(devices, slots, values, rows)
    received = lax.all_to_all(sending, ("dom", "sub"), split_axis=0, concat_axis=0, tiled=True)
    received = received.reshape(devices * slots, values, rows)
    targets = relay_target[0].reshape(-1)
    order, same, last, have = target_order(targets, new_count)
    return mass_solve(
        order, same, last, have, coupling, received, mass_diag, mass_next, precond
    )


def solution(mesh):
    whole = ("dom", "sub")
    placed = (
        P(whole, None, None),
        P(whole, None, None),
        P(whole, None),
        P(whole, None, None),
        P(whole, None, None),
        P(whole, None, None),
        P(whole, None, None),
        P(whole, None, None),
        P(whole),
        P(whole, None, None),
    )
    return jax.shard_map(
        body,
        mesh=mesh,
        in_specs=placed,
        out_specs=(P(whole, None, None), P(whole, None, None)),
        check_vma=False,
    )
```

time: 616 us -> 229 us (0.37)
  blocking collectives: 328 us -> 0 us
  Pallas kernels: 0 us -> 108 us
  matrix products: 101 us -> 5.34 us
  other arithmetic: 47.6 us -> 5.66 us
  starting transfers between devices: 35 us -> 17.5 us
    psum x5 -> x0, blocking collectives: 328 us -> none  [the longest x3 195 us: squares(): return lax.psum(local_inner(residual, reduced), ('dom', 'sub'))]
    pallas_call x0 -> x1, Pallas kernels: none -> 108 us  [mass_solve(): pl.pallas_call(kernel, out_shape=(field, field), in_specs=[smem] * 5 + [h...]
    dot_general x14 -> x1, matrix products: 101 us -> 5.34 us  [body(): jnp.einsum('dcvs,dcsr->dcvr', arrived, mixing, preferred_element_type=F32)]
    reduce_sum x5 -> x3, other arithmetic: 22.5 us -> 0.91 us  [the longest x1 0.64 us: target_order(): ordered = jnp.sum(jnp.where(at, targets[None, :], 0), axis=1)]
    ppermute x6 -> x0, starting transfers between devices: 17.1 us -> none  [shifted(): lax.ppermute(value, axis, [(source, source + steps) for source in range(f...]
    sub x3 -> x0, other arithmetic: 10.2 us -> none  [body(): residual = residual - alpha[None, :, None] * image]
    add x2 -> x1, other arithmetic: 7.82 us -> 0.01 us  [target_order(): key = targets * slots + spot]
  transfers between devices with their start and end apart: 8 -> 2, of which waited for: 2 -> 2; matrix products, arithmetic and copies ran while one was open for 7% -> 1% of each run, Pallas kernels for 0% -> 0%
where the time goes in v1:
time: 229 us; the launch traced here: 228 us
  Pallas kernels  108 us (47%)
  waiting for transfers between devices  79.7 us (35%)
  starting transfers between devices  17.5 us (8%)
  local copies, waits for them, and re-layouts  10.6 us (5%)
  other arithmetic  5.66 us (2%)
  matrix products  5.34 us (2%)
    pallas_call x1, Pallas kernels, mass_solve(): pl.pallas_call(kernel, out_shape=(field, field), in_specs=[smem] * 5 + [h...  108 us
    all_to_all x1, waiting for transfers between devices, body(): lax.all_to_all(sending, ('dom', 'sub'), split_axis=0, concat_axis=0, tile...  49.6 us
    all_to_all x1, waiting for transfers between devices, body(): lax.all_to_all(outgoing, ('dom', 'sub'), split_axis=0, concat_axis=0, til...  30.1 us
    all_to_all x1, starting transfers between devices, body(): lax.all_to_all(outgoing, ('dom', 'sub'), split_axis=0, concat_axis=0, til...  11.5 us
    all_to_all x1, starting transfers between devices, body(): lax.all_to_all(sending, ('dom', 'sub'), split_axis=0, concat_axis=0, tile...  6.06 us
    dot_general x1, matrix products, body(): jnp.einsum('dcvs,dcsr->dcvr', arrived, mixing, preferred_element_type=F32)  5.34 us
    gather x1, local copies, waits for them, and re-layouts, body(): flat_tiles[relay_list[0].reshape(-1)].reshape(devices, slots, values, rows)  4.97 us
    unnamed x10, local copies, waits for them, and re-layouts  4.65 us
  transfers between devices with their start and end apart: 2, of which 2 were waited for; matrix products, arithmetic and copies ran while one was open for 1% of the time, Pallas kernels for 0%

profile of v1, /device:TPU:1, one launch (start us, length us, event | category | flops | bytes accessed | tf_op | source)
XLA Modules:
  0.0 227.9 jit_solution(8668742721405225645)
XLA Ops:
  0.6 0.0 copy-start
  0.6 0.7 fusion.3
  1.4 0.7 compare_bitcast_fusion
  2.0 0.0 copy-done
  2.0 1.0 gather_fusion
  3.0 1.5 bitcast_select_fusion
  4.5 0.0 copy-start.3
  4.5 11.5 %all-to-all-start = ((bf16[128,1,64,128]{3,2,1,0:T(8,128)(2,1)}), bf16[128,1,64,128]{3,2,1,0:T(8,128)(2,1)S(1)}, u32[]{:S(2)}, u32[]{:S(2)}) async-start(bf16[128,1,64,128]{3,2,1,0:T(8,128)(2,1)} %bitcast_select_fusion), calls=%async_computation | async-start | bytes 4194304 | tf_op jit(solution)/shard_map/all_to_all | solution.py:460
  16.0 0.0 copy-done.3
  16.1 30.1 %all-to-all-done = bf16[128,1,64,128]{3,2,1,0:T(8,128)(2,1)S(1)} async-done(((bf16[128,1,64,128]{3,2,1,0:T(8,128)(2,1)}), bf16[128,1,64,128]{3,2,1,0:T(8,128)(2,1)S(1)}, u32[]{:S(2)}, u32[]{:S(2)}) %all-to-all-start) | async-done | bytes 2097184 | tf_op jit(solution)/shard_map/all_to_all | solution.py:460
  46.1 5.3 %fusion = f32[128,64,128]{2,1,0:T(8,128)} fusion(bf16[128,128,128]{2,1,0:T(8,128)(2,1)} %param.13, bf16[128,1,64,128]{3,2,1,0:T(8,128)(2,1)S(1)} %all-to-all-done), kind=kOutput, calls=%fused_computation.2 | convolution fusion | flops 268435456 | bytes 10485760 | tf_op jit(solution)/shard_map/dcvs,dcsr->dcvr/dot_general | solution.py:462
  51.5 5.0 %gather_fusion.1 = f32[128,64,128]{2,1,0:T(8,128)} fusion(f32[128,64,128]{2,1,0:T(8,128)} %fusion, s32[1024]{0:T(1024)S(1)} %pad_clamp_fusion), kind=kCustom, calls=%fused_computation.1 | custom fusion | bytes 8389120 | tf_op jit(solution)/shard_map/gather | solution.py:464
  56.4 0.0 copy-start.2
  56.4 6.1 %all-to-all-start.1 = ((f32[128,1,64,128]{3,2,1,0:T(8,128)}), f32[128,1,64,128]{3,2,1,0:T(8,128)}, u32[]{:S(2)}, u32[]{:S(2)}) async-start(f32[128,1,64,128]{3,2,1,0:T(8,128)} %bitcast.22), calls=%async_computation.1 | async-start | bytes 8388608 | tf_op jit(solution)/shard_map/all_to_all | solution.py:465
  62.5 0.0 copy-done.2
  62.5 0.1 fusion.2
  62.6 0.5 convert_element_type.12.refs_3_
  63.2 0.2 convert_reduce_fusion
  63.4 0.6 select_reduce_fusion
  64.0 0.1 slice_compare_fusion
  64.1 0.6 add_convert_fusion.refs_1_
  64.7 0.1 convert_reduce_fusion.1
  64.8 0.5 add_maximum_fusion.refs_2_
  65.3 49.6 %all-to-all-done.1 = f32[128,1,64,128]{3,2,1,0:T(8,128)} async-done(((f32[128,1,64,128]{3,2,1,0:T(8,128)}), f32[128,1,64,128]{3,2,1,0:T(8,128)}, u32[]{:S(2)}, u32[]{:S(2)}) %all-to-all-start.1) | async-done | bytes 4194336 | tf_op jit(solution)/shard_map/all_to_all | solution.py:465
  114.9 108.4 %shard_map.113 = (f32[64,64,128]{2,1,0:T(8,128)}, f32[64,64,128]{2,1,0:T(8,128)}) custom-call(s32[128]{0:T(128)} %get-tuple-element.3.refs_0_, f32[128]{0:T(128)} %add_convert_fusion.refs_1_, s32[64]{0:T(128)} %add_maximum_fusion.refs_2_, f32[64]{0:T(128)} %convert_element_type.12.refs_3_, s32[64]{0:T(128)} %refs_4_.1, f32[128,64,128]{2,1,0:T(8,128)} %bitcast.10.refs_5_, ...), custom_call_target="tpu_custom_call" | custom-call | tf_op jit(solution)/shard_map/pallas_call | solution.py:385
  223.2 0.0 copy-start.1
  223.2 3.3 %copy.16 = f32[64,64,128]{2,1,0:T(8,128)} copy(f32[64,64,128]{2,1,0:T(8,128)} %get-tuple-element.6) | data formatting | bytes 4194304
  226.6 0.0 copy-done.1
  226.6 1.3 copy.17
  (4 shorter events, 0.0 us)
Async XLA Ops:
  0.6 1.4 copy-start
  4.5 11.5 %copy-start.3 = (s32[1,128,1]{1,2,0:T(1,128)S(1)}, s32[1,128,1]{1,2,0:T(1,128)}, u32[]{:S(2)}) copy-start(s32[1,128,1]{1,2,0:T(1,128)} %param.14) | copy-start | bytes 1540
  4.5 41.6 %all-to-all-start = ((bf16[128,1,64,128]{3,2,1,0:T(8,128)(2,1)}), bf16[128,1,64,128]{3,2,1,0:T(8,128)(2,1)S(1)}, u32[]{:S(2)}, u32[]{:S(2)}) async-start(bf16[128,1,64,128]{3,2,1,0:T(8,128)(2,1)} %bitcast_select_fusion), calls=%async_computation | async-start | bytes 4194304 | tf_op jit(solution)/shard_map/all_to_all | solution.py:460
  56.4 6.1 %copy-start.2 = (s32[1,128,1]{1,2,0:T(1,128)S(1)}, s32[1,128,1]{1,2,0:T(1,128)}, u32[]{:S(2)}) copy-start(s32[1,128,1]{1,2,0:T(1,128)} %param.15) | copy-start | bytes 1540
  56.4 58.4 %all-to-all-start.1 = ((f32[128,1,64,128]{3,2,1,0:T(8,128)}), f32[128,1,64,128]{3,2,1,0:T(8,128)}, u32[]{:S(2)}, u32[]{:S(2)}) async-start(f32[128,1,64,128]{3,2,1,0:T(8,128)} %bitcast.22), calls=%async_computation.1 | async-start | bytes 8388608 | tf_op jit(solution)/shard_map/all_to_all | solution.py:465
  223.2 3.3 %copy-start.1 = (f32[64,64,128]{2,1,0:T(8,128)S(1)}, f32[64,64,128]{2,1,0:T(8,128)}, u32[]{:S(2)}) copy-start(f32[64,64,128]{2,1,0:T(8,128)} %get-tuple-element.7) | copy-start | bytes 6291460

commit v2 on v1

--- a/solution.py
+++ b/solution.py
@@ -10,6 +10,8 @@
 BF16 = jnp.bfloat16
 STEPS = 3
 CHUNK = 4
+ORDER = 37
+DIGITS = ((4, 32), (4, 8), (4, 2), (2, 1))
 
 
 def split(value):
@@ -36,12 +38,21 @@
     last_ref,
     have_ref,
     links_ref,
-    tiles_hbm,
+    pick_ref,
+    live_ref,
+    relay_ref,
+    hist_hbm,
+    mixed_hbm,
     diag_hbm,
     next_hbm,
     prec_hbm,
     x_hbm,
     res_hbm,
+    hist,
+    mixed,
+    out_a,
+    in_a,
+    out_b,
     tiles,
     stage,
     wa,
@@ -58,7 +69,12 @@
     red_src,
     red_dom,
     red_sub,
-    tile_sem,
+    hist_sem,
+    mixed_sem,
+    a_send,
+    a_recv,
+    b_send,
+    b_recv,
     stage_sem,
     halo_send,
     halo_recv,
@@ -79,24 +95,50 @@
     after_id = (after // subs, lax.rem(after, subs))
     before_id = (before // subs, lax.rem(before, subs))
 
-    load_tiles = pltpu.make_async_copy(tiles_hbm, tiles, tile_sem)
-    load_tiles.start()
+    load_hist = pltpu.make_async_copy(hist_hbm, hist, hist_sem)
+    load_hist.start()
+    load_mixed = pltpu.make_async_copy(mixed_hbm, mixed, mixed_sem)
+
+    def peer_of(s):
+        place = lax.rem(s * ORDER, devices)
+        there = 0
+        for size, stride in DIGITS:
+            mine = lax.rem(me // stride, size)
+            there += lax.rem(mine + lax.rem(place // stride, size), size) * stride
+        return there
+
+    def id_of(peer):
+        return (peer // subs, lax.rem(peer, subs))
 
     barrier = pltpu.get_barrier_semaphore()
-    pl.semaphore_signal(barrier, inc=1, device_id=after_id, device_id_type=MESH)
-    pl.semaphore_signal(barrier, inc=1, device_id=before_id, device_id_type=MESH)
-
-    @pl.loop(1, doms)
-    def _(j):
-        pl.semaphore_signal(
-            barrier, inc=1, device_id=(lax.rem(me_dom + j, doms), me_sub), device_id_type=MESH
-        )
-
-    @pl.loop(1, subs)
-    def _(j):
-        pl.semaphore_signal(
-            barrier, inc=1, device_id=(me_dom, lax.rem(me_sub + j, subs)), device_id_type=MESH
-        )
+
+    @pl.loop(1, devices)
+    def _(s):
+        pl.semaphore_signal(barrier, inc=1, device_id=id_of(peer_of(s)), device_id_type=MESH)
+
+    load_hist.wait()
+
+    @pl.loop(0, devices)
+    def _(e):
+        block = hist[pick_ref[e]]
+        out_a[e] = jnp.where(live_ref[e] > 0, block, jnp.zeros_like(block))
+
+    pl.semaphore_wait(barrier, devices - 1)
+
+    @pl.loop(1, devices)
+    def _(s):
+        peer = peer_of(s)
+        pltpu.make_async_remote_copy(
+            src_ref=out_a.at[peer],
+            dst_ref=in_a.at[me],
+            send_sem=a_send,
+            recv_sem=a_recv,
+            device_id=id_of(peer),
+            device_id_type=MESH,
+        ).start()
+
+    in_a[me] = out_a[me]
+    load_mixed.start()
 
     sources = (diag_hbm, next_hbm, prec_hbm)
 
@@ -152,8 +194,6 @@
             wp[g, :, 0:rows] = high
             wp[g, :, rows : 2 * rows] = low
 
-    pl.semaphore_wait(barrier, 2 + doms - 1 + subs - 1)
-
     def reduce_over(phase, value):
         def dom_copy(peer, slot):
             return pltpu.make_async_remote_copy(
@@ -229,8 +269,40 @@
     theta = jnp.sum(jnp.sum(theta, axis=0, keepdims=True), axis=1, keepdims=True)
     inv[...] = jnp.broadcast_to((1.0 * devices * count * rows) / theta, inv.shape)
 
-    load_tiles.wait()
-    acc[0] = jnp.zeros_like(acc[0])
+    others = pl.ds(0, devices - 1)
+    load_mixed.wait()
+    pltpu.make_async_copy(in_a.at[others], in_a.at[others], a_recv).wait()
+
+    def mixed_tile(peer):
+        spot = relay_ref[peer]
+        return jnp.dot(in_a[spot], mixed[spot], preferred_element_type=F32)
+
+    def send_tile(s):
+        peer = peer_of(s)
+        pltpu.make_async_remote_copy(
+            src_ref=out_b.at[peer],
+            dst_ref=tiles.at[me],
+            send_sem=b_send,
+            recv_sem=b_recv,
+            device_id=id_of(peer),
+            device_id_type=MESH,
+        ).start()
+
+    @pl.loop(1, devices)
+    def _(s):
+        peer = peer_of(s)
+        out_b[peer] = mixed_tile(peer)
+
+        @pl.when(s > 1)
+        def _():
+            send_tile(s - 1)
+
+    tiles[me] = mixed_tile(me)
+    send_tile(devices - 1)
+    pltpu.make_async_copy(out_a.at[others], out_a.at[others], a_send).wait()
+    pltpu.make_async_copy(out_b.at[others], out_b.at[others], b_send).wait()
+    pltpu.make_async_copy(tiles.at[others], tiles.at[others], b_recv).wait()
+
 
     def add_tile(j, running):
         running = running * same_ref[j] + tiles[order_ref[j]]
@@ -369,9 +441,10 @@
     put_r.wait()
 
 
-def mass_solve(order, same, last, have, links, tiles, mass_diag, mass_next, precond):
+def mass_solve(order, same, last, have, links, pick, live, relay, history, mixed, mass_diag, mass_next, precond):
     doms, subs = lax.axis_size("dom"), lax.axis_size("sub")
-    slots, values, rows = tiles.shape
+    slots = mixed.shape[0]
+    blocks, values, rows = history.shape
     count = mass_diag.shape[0]
     shape = (doms, subs, count, values, rows, slots)
 
@@ -385,9 +458,14 @@
     return pl.pallas_call(
         kernel,
         out_shape=(field, field),
-        in_specs=[smem] * 5 + [hbm] * 4,
+        in_specs=[smem] * 8 + [hbm] * 5,
         out_specs=(hbm, hbm),
         scratch_shapes=[
+            pltpu.VMEM((blocks, values, rows), BF16),
+            pltpu.VMEM((slots, rows, rows), BF16),
+            pltpu.VMEM((slots, values, rows), BF16),
+            pltpu.VMEM((slots, values, rows), BF16),
+            pltpu.VMEM((slots, values, rows), F32),
             pltpu.VMEM((slots, values, rows), F32),
             pltpu.VMEM((2, 3, CHUNK, rows, rows), F32),
             pltpu.VMEM((count + 1, 3 * rows, 2 * rows), BF16),
@@ -405,6 +483,11 @@
             pltpu.VMEM((2, doms, 8, rows), F32),
             pltpu.VMEM((2, subs, 8, rows), F32),
             dma,
+            dma,
+            dma,
+            dma,
+            dma,
+            dma,
             dma((2, 3)),
             dma((STEPS, 2)),
             dma((STEPS, 2)),
@@ -419,7 +502,7 @@
         compiler_params=pltpu.CompilerParams(
             collective_id=0, has_side_effects=True, vmem_limit_bytes=60 * 1024 * 1024
         ),
-    )(order, same, last, have, links, tiles, mass_diag, mass_next, precond)
+    )(order, same, last, have, links, pick, live, relay, history, mixed, mass_diag, mass_next, precond)
 
 
 def target_order(targets, count):
@@ -449,25 +532,23 @@
     coupling,
     precond,
 ):
-    devices = lax.axis_size(("dom", "sub"))
-    slots = send_list.shape[2]
-    values = history.shape[1]
-    rows = history.shape[2]
     new_count = mass_diag.shape[0]
-    picks = send_list[0]
-    live = jnp.arange(slots, dtype=jnp.int32)[None, :] < send_count[0][:, None]
-    outgoing = jnp.where(live[:, :, None, None], history[picks], jnp.zeros((), BF16))
-    arrived = lax.all_to_all(outgoing, ("dom", "sub"), split_axis=0, concat_axis=0, tiled=True)
-    mixing = mixed_mass.reshape(devices, slots, rows, rows)
-    tiles = jnp.einsum("dcvs,dcsr->dcvr", arrived, mixing, preferred_element_type=F32)
-    flat_tiles = tiles.reshape(devices * slots, values, rows)
-    sending = flat_tiles[relay_list[0].reshape(-1)].reshape(devices, slots, values, rows)
-    received = lax.all_to_all(sending, ("dom", "sub"), split_axis=0, concat_axis=0, tiled=True)
-    received = received.reshape(devices * slots, values, rows)
-    targets = relay_target[0].reshape(-1)
+    targets = relay_target.reshape(-1)
     order, same, last, have = target_order(targets, new_count)
     return mass_solve(
-        order, same, last, have, coupling, received, mass_diag, mass_next, precond
+        order,
+        same,
+        last,
+        have,
+        coupling,
+        send_list.reshape(-1),
+        send_count.reshape(-1),
+        relay_list.reshape(-1),
+        history,
+        mixed_mass,
+        mass_diag,
+        mass_next,
+        precond,
     )
 
 

time: 229 us -> 191 us (0.83)
  waiting for transfers between devices: 79.7 us -> 0 us
  Pallas kernels: 108 us -> 180 us
  starting transfers between devices: 17.5 us -> 0 us
  local copies, waits for them, and re-layouts: 10.6 us -> 4.63 us
  matrix products: 5.34 us -> 0 us
    all_to_all x2 -> x0, waiting for transfers between devices: 79.7 us -> none  [the longest x1 49.6 us: body(): lax.all_to_all(sending, ('dom', 'sub'), split_axis=0, concat_axis=0, tile...]
    pallas_call x1, Pallas kernels: 108 us -> 180 us  [mass_solve(): pl.pallas_call(kernel, out_shape=(field, field), in_specs=[smem] * 8 + [h...]
    all_to_all x2 -> x0, starting transfers between devices: 17.5 us -> none  [the longest x1 11.5 us: body(): lax.all_to_all(outgoing, ('dom', 'sub'), split_axis=0, concat_axis=0, til...]
    gather x2 -> x0, local copies, waits for them, and re-layouts: 5.92 us -> none  [the longest x1 4.97 us: body(): flat_tiles[relay_list[0].reshape(-1)].reshape(devices, slots, values, rows)]
    dot_general x1 -> x0, matrix products: 5.34 us -> none  [body(): jnp.einsum('dcvs,dcsr->dcvr', arrived, mixing, preferred_element_type=F32)]
    unnamed x10 -> x4, local copies, waits for them, and re-layouts: 4.65 us -> 4.63 us
  transfers between devices with their start and end apart: 2 -> 0, of which waited for: 2 -> 0; matrix products, arithmetic and copies ran while one was open for 1% -> 0% of each run, Pallas kernels for 0% -> 0%
where the time goes in v2:
time: 191 us; the launch traced here: 190 us
  Pallas kernels  180 us (94%)
  other arithmetic  5.4 us (3%)
  local copies, waits for them, and re-layouts  4.63 us (2%)
    pallas_call x1, Pallas kernels, mass_solve(): pl.pallas_call(kernel, out_shape=(field, field), in_specs=[smem] * 8 + [h...  180 us
    unnamed x4, local copies, waits for them, and re-layouts  4.63 us

profile of v2, /device:TPU:1, one launch (start us, length us, event | category | flops | bytes accessed | tf_op | source)
XLA Modules:
  0.0 190.5 jit_solution(7328967516729882066)
XLA Ops:
  0.6 0.8 convert_reduce_fusion.1
  1.4 0.5 add_maximum_fusion.refs_2_
  1.9 0.8 fusion
  2.7 0.6 convert_element_type.12.refs_3_
  3.3 0.7 iota_add_fusion
  3.9 0.2 convert_reduce_fusion
  4.1 1.3 select_reduce_fusion
  5.4 0.1 slice_compare_fusion
  5.5 0.6 add_convert_fusion.refs_1_
  6.0 179.8 %shard_map.113 = (f32[64,64,128]{2,1,0:T(8,128)}, f32[64,64,128]{2,1,0:T(8,128)}) custom-call(s32[128]{0:T(128)} %get-tuple-element.3.refs_0_, f32[128]{0:T(128)} %add_convert_fusion.refs_1_, s32[64]{0:T(128)} %add_maximum_fusion.refs_2_, f32[64]{0:T(128)} %convert_element_type.12.refs_3_, s32[64]{0:T(128)} %refs_4_.1, s32[128]{0:T(128)} %bitcast.5, ...), custom_call_target="tpu_custom_call" | custom-call | tf_op jit(solution)/shard_map/pallas_call | solution.py:458
  185.9 0.0 copy-start
  185.9 3.3 %copy.14 = f32[64,64,128]{2,1,0:T(8,128)} copy(f32[64,64,128]{2,1,0:T(8,128)} %get-tuple-element.6) | data formatting | bytes 4194304
  189.2 0.0 copy-done
  189.2 1.3 copy.15
Async XLA Ops:
  185.9 3.3 %copy-start = (f32[64,64,128]{2,1,0:T(8,128)S(1)}, f32[64,64,128]{2,1,0:T(8,128)}, u32[]{:S(2)}) copy-start(f32[64,64,128]{2,1,0:T(8,128)} %get-tuple-element.7) | copy-start | bytes 6291460

commit v3 on v2

--- a/solution.py
+++ b/solution.py
@@ -11,7 +11,7 @@
 STEPS = 3
 CHUNK = 4
 ORDER = 37
-DIGITS = ((4, 32), (4, 8), (4, 2), (2, 1))
+FIRST_BITS = 0b0101010
 
 
 def split(value):
@@ -69,6 +69,7 @@
     red_src,
     red_dom,
     red_sub,
+    enter,
     hist_sem,
     mixed_sem,
     a_send,
@@ -100,21 +101,29 @@
     load_mixed = pltpu.make_async_copy(mixed_hbm, mixed, mixed_sem)
 
     def peer_of(s):
-        place = lax.rem(s * ORDER, devices)
-        there = 0
-        for size, stride in DIGITS:
-            mine = lax.rem(me // stride, size)
-            there += lax.rem(mine + lax.rem(place // stride, size), size) * stride
-        return there
+        place = (s * ORDER) & (devices - 1)
+        carry = (place & me & FIRST_BITS) << 1
+        return place ^ me ^ carry
 
     def id_of(peer):
-        return (peer // subs, lax.rem(peer, subs))
+        return (peer >> 3, peer & (subs - 1))
+
+    width = 4
+    me_y, me_x = me_dom >> 2, me_dom & (width - 1)
+
+    def line_x(j):
+        return (me_y * width + ((me_x + j) & (width - 1)), me_sub)
+
+    def line_y(j):
+        return (((me_y + j) & (width - 1)) * width + me_x, me_sub)
 
     barrier = pltpu.get_barrier_semaphore()
-
-    @pl.loop(1, devices)
-    def _(s):
-        pl.semaphore_signal(barrier, inc=1, device_id=id_of(peer_of(s)), device_id_type=MESH)
+    for j in range(1, subs):
+        other = (me_dom, (me_sub + j) & (subs - 1))
+        pl.semaphore_signal(barrier, inc=1, device_id=other, device_id_type=MESH)
+    for j in range(1, width):
+        pl.semaphore_signal(barrier, inc=1, device_id=line_x(j), device_id_type=MESH)
+        pl.semaphore_signal(barrier, inc=1, device_id=line_y(j), device_id_type=MESH)
 
     load_hist.wait()
 
@@ -123,7 +132,13 @@
         block = hist[pick_ref[e]]
         out_a[e] = jnp.where(live_ref[e] > 0, block, jnp.zeros_like(block))
 
-    pl.semaphore_wait(barrier, devices - 1)
+    pl.semaphore_wait(barrier, subs - 1 + 2 * (width - 1))
+    for j in range(1, width):
+        pl.semaphore_signal(enter.at[0], inc=1, device_id=line_x(j), device_id_type=MESH)
+    pl.semaphore_wait(enter.at[0], width - 1)
+    for j in range(1, width):
+        pl.semaphore_signal(enter.at[1], inc=1, device_id=line_y(j), device_id_type=MESH)
+    pl.semaphore_wait(enter.at[1], width - 1)
 
     @pl.loop(1, devices)
     def _(s):
@@ -277,8 +292,7 @@
         spot = relay_ref[peer]
         return jnp.dot(in_a[spot], mixed[spot], preferred_element_type=F32)
 
-    def send_tile(s):
-        peer = peer_of(s)
+    def send_tile(peer):
         pltpu.make_async_remote_copy(
             src_ref=out_b.at[peer],
             dst_ref=tiles.at[me],
@@ -288,17 +302,18 @@
             device_id_type=MESH,
         ).start()
 
-    @pl.loop(1, devices)
-    def _(s):
+    first = peer_of(1)
+    out_b[first] = mixed_tile(first)
+
+    def next_tile(s, ready):
         peer = peer_of(s)
         out_b[peer] = mixed_tile(peer)
-
-        @pl.when(s > 1)
-        def _():
-            send_tile(s - 1)
-
+        send_tile(ready)
+        return peer
+
+    ready = lax.fori_loop(2, devices, next_tile, first)
     tiles[me] = mixed_tile(me)
-    send_tile(devices - 1)
+    send_tile(ready)
     pltpu.make_async_copy(out_a.at[others], out_a.at[others], a_send).wait()
     pltpu.make_async_copy(out_b.at[others], out_b.at[others], b_send).wait()
     pltpu.make_async_copy(tiles.at[others], tiles.at[others], b_recv).wait()
@@ -315,36 +330,59 @@
     def _(g):
         res[0, g] = red[last_ref[g]] * have_ref[g]
 
-    def precondition(g, k, value):
-        out = product(stacked(value), wp[g], values) + value * diag_p[g]
-        red[k * count + g] = out
-        xs[k % 2, g + 1] = stacked(out)
-
-    def apply_block(g, k, left, right):
-        here = xs[k % 2, g + 1]
-        image = product(jnp.concatenate([here, right, left], axis=1), wa[g], values)
-        field = red[k * count + g]
-        image = image + field * diag_a[g]
-        now = res[k, g]
-        later = now - image * inv[0:1]
-        res[k + 1, g] = later
-        step = now - later
+    def precondition(blocks, k, fields):
+        outs = [
+            product(stacked(field), wp[g], values) + field * diag_p[g]
+            for g, field in zip(blocks, fields)
+        ]
+        for g, out in zip(blocks, outs):
+            red[k * count + g] = out
+            xs[k % 2, g + 1] = stacked(out)
+
+    def apply_blocks(blocks, k, operands):
+        fields = [red[k * count + g] for g in blocks]
+        nows = [res[k, g] for g in blocks]
+        befores = [res[k - 1, g] for g in blocks] if k > 0 else None
+        images = [
+            product(operand, wa[g], values) + field * diag_a[g]
+            for g, field, operand in zip(blocks, fields, operands)
+        ]
+        laters = [now - image * inv[0:1] for now, image in zip(nows, images)]
+        steps = [now - later for now, later in zip(nows, laters)]
+
+        def dots(slot, left, right):
+            acc[slot] += sum(a * b for a, b in zip(left, right))
+
+        if k + 1 < STEPS:
+            precondition(blocks, k + 1, laters)
+        for g, later in zip(blocks, laters):
+            res[k + 1, g] = later
         if k == 0:
-            acc[0] += field * step
-        if k == 1:
-            acc[1] += field * (res[0, g] - now)
-            acc[2] += field * step
+            dots(0, fields, steps)
+        else:
+            dots(2 * k - 1, fields, [x - y for x, y in zip(befores, nows)])
+            dots(2 * k, fields, steps)
         if k == 2:
-            acc[3] += field * (res[1, g] - now)
-            acc[4] += field * step
-            acc[5] += red[g] * later
-            acc[6] += red[count + g] * later
-            acc[7] += field * later
-        if k + 1 < STEPS:
-            precondition(g, k + 1, later)
+            dots(5, [red[g] for g in blocks], laters)
+            dots(6, [red[count + g] for g in blocks], laters)
+            dots(7, fields, laters)
 
     def inner(g, k):
-        apply_block(g, k, xs[k % 2, g], xs[k % 2, g + 2])
+        near = [xs[k % 2, g + i] for i in range(4)]
+        apply_blocks(
+            (g, g + 1), k, [jnp.concatenate([near[i + 1], near[i + 2], near[i]], axis=1) for i in range(2)]
+        )
+
+    def inners(start, stop, k):
+        @pl.loop(0, (stop - start) // 2)
+        def _(i):
+            inner(start + 2 * i, k)
+
+    def preconditions(start, stop):
+        @pl.loop(0, (stop - start) // 2)
+        def _(i):
+            g = start + 2 * i
+            precondition((g, g + 1), 0, (res[0, g], res[0, g + 1]))
 
     def halo_copy(k, side):
         return pltpu.make_async_remote_copy(
@@ -356,45 +394,34 @@
             device_id_type=MESH,
         )
 
-    middle = count // 2
+    edges = (0, count - 1)
+    middle = count // 2 + 1
     acc[...] = jnp.zeros_like(acc)
-    precondition(0, 0, res[0, 0])
-    precondition(count - 1, 0, res[0, count - 1])
-
-    @pl.loop(1, 9)
-    def _(g):
-        precondition(g, 0, res[0, g])
-
+    precondition(edges, 0, [res[0, g] for g in edges])
+    preconditions(1, 9)
     halo_copy(0, 0).start()
     halo_copy(0, 1).start()
-
-    @pl.loop(9, count - 1)
-    def _(g):
-        precondition(g, 0, res[0, g])
+    preconditions(9, count - 1)
 
     link_copy.wait()
     for k in range(STEPS):
-
-        @pl.loop(1, middle)
-        def _(g):
-            inner(g, k)
-
+        inners(1, middle, k)
         halo_copy(k, 0).wait()
         halo_copy(k, 1).wait()
-        apply_block(0, k, halo[k, 0], xs[k % 2, 2])
-        apply_block(count - 1, k, xs[k % 2, count - 1], halo[k, 1])
-
-        @pl.loop(middle, middle + 4)
-        def _(g):
-            inner(g, k)
-
+        buf = k % 2
+        apply_blocks(
+            edges,
+            k,
+            [
+                jnp.concatenate([xs[buf, 1], xs[buf, 2], halo[k, 0]], axis=1),
+                jnp.concatenate([xs[buf, count], halo[k, 1], xs[buf, count - 1]], axis=1),
+            ],
+        )
+        inners(middle, middle + 4, k)
         if k + 1 < STEPS:
             halo_copy(k + 1, 0).start()
             halo_copy(k + 1, 1).start()
-
-        @pl.loop(middle + 4, count - 1)
-        def _(g):
-            inner(g, k)
+        inners(middle + 4, count - 1, k)
 
     lane = lax.broadcasted_iota(jnp.int32, (values, rows), 1)
     packed = jnp.zeros((values, rows), F32)
@@ -482,6 +509,7 @@
             pltpu.VMEM((2, 2, 8, rows), F32),
             pltpu.VMEM((2, doms, 8, rows), F32),
             pltpu.VMEM((2, subs, 8, rows), F32),
+            pltpu.SemaphoreType.REGULAR((2,)),
             dma,
             dma,
             dma,

time: 191 us -> 157 us (0.82)
  Pallas kernels: 180 us -> 146 us
    pallas_call x1, Pallas kernels: 180 us -> 146 us  [mass_solve(): pl.pallas_call(kernel, out_shape=(field, field), in_specs=[smem] * 8 + [h...]
where the time goes in v3:
time: 157 us
  Pallas kernels  146 us (93%)
  other arithmetic  5.4 us (3%)
  local copies, waits for them, and re-layouts  4.63 us (3%)
    pallas_call x1, Pallas kernels, mass_solve(): pl.pallas_call(kernel, out_shape=(field, field), in_specs=[smem] * 8 + [h...  146 us
    unnamed x4, local copies, waits for them, and re-layouts  4.63 us

profile of v3, /device:TPU:1, one launch (start us, length us, event | category | flops | bytes accessed | tf_op | source)
XLA Modules:
  0.0 156.7 jit_solution(14530152315726984482)
XLA Ops:
  0.6 0.8 convert_reduce_fusion.1
  1.4 0.5 add_maximum_fusion.refs_2_
  1.9 0.8 fusion
  2.7 0.6 convert_element_type.12.refs_3_
  3.3 0.7 iota_add_fusion
  3.9 0.2 convert_reduce_fusion
  4.1 1.3 select_reduce_fusion
  5.4 0.1 slice_compare_fusion
  5.5 0.6 add_convert_fusion.refs_1_
  6.0 146.0 %shard_map.113 = (f32[64,64,128]{2,1,0:T(8,128)}, f32[64,64,128]{2,1,0:T(8,128)}) custom-call(s32[128]{0:T(128)} %get-tuple-element.3.refs_0_, f32[128]{0:T(128)} %add_convert_fusion.refs_1_, s32[64]{0:T(128)} %add_maximum_fusion.refs_2_, f32[64]{0:T(128)} %convert_element_type.12.refs_3_, s32[64]{0:T(128)} %refs_4_.1, s32[128]{0:T(128)} %bitcast.5, ...), custom_call_target="tpu_custom_call" | custom-call | tf_op jit(solution)/shard_map/pallas_call | solution.py:485
  152.0 0.0 copy-start
  152.0 3.3 %copy.14 = f32[64,64,128]{2,1,0:T(8,128)} copy(f32[64,64,128]{2,1,0:T(8,128)} %get-tuple-element.6) | data formatting | bytes 4194304
  155.3 0.0 copy-done
  155.3 1.3 copy.15
Async XLA Ops:
  152.0 3.3 %copy-start = (f32[64,64,128]{2,1,0:T(8,128)S(1)}, f32[64,64,128]{2,1,0:T(8,128)}, u32[]{:S(2)}) copy-start(f32[64,64,128]{2,1,0:T(8,128)} %get-tuple-element.7) | copy-start | bytes 6291460

commit v4 on v3

--- a/solution.py
+++ b/solution.py
@@ -11,6 +11,9 @@
 STEPS = 3
 CHUNK = 4
 ORDER = 37
+GROUP = 4
+BATCH = 8
+LEVELS = 32767.0
 FIRST_BITS = 0b0101010
 
 
@@ -33,10 +36,7 @@
 
 def solve_kernel(
     shape,
-    order_ref,
-    same_ref,
-    last_ref,
-    have_ref,
+    target_ref,
     links_ref,
     pick_ref,
     live_ref,
@@ -54,6 +54,8 @@
     in_a,
     out_b,
     tiles,
+    unit_out,
+    unit_in,
     stage,
     wa,
     wp,
@@ -69,6 +71,9 @@
     red_src,
     red_dom,
     red_sub,
+    rank_rows,
+    table,
+    table_sem,
     enter,
     hist_sem,
     mixed_sem,
@@ -76,6 +81,8 @@
     a_recv,
     b_send,
     b_recv,
+    c_send,
+    c_recv,
     stage_sem,
     halo_send,
     halo_recv,
@@ -125,19 +132,20 @@
         pl.semaphore_signal(barrier, inc=1, device_id=line_x(j), device_id_type=MESH)
         pl.semaphore_signal(barrier, inc=1, device_id=line_y(j), device_id_type=MESH)
 
-    load_hist.wait()
-
-    @pl.loop(0, devices)
-    def _(e):
-        block = hist[pick_ref[e]]
-        out_a[e] = jnp.where(live_ref[e] > 0, block, jnp.zeros_like(block))
-
     pl.semaphore_wait(barrier, subs - 1 + 2 * (width - 1))
     for j in range(1, width):
         pl.semaphore_signal(enter.at[0], inc=1, device_id=line_x(j), device_id_type=MESH)
     pl.semaphore_wait(enter.at[0], width - 1)
     for j in range(1, width):
         pl.semaphore_signal(enter.at[1], inc=1, device_id=line_y(j), device_id_type=MESH)
+
+    load_hist.wait()
+
+    @pl.loop(0, devices)
+    def _(e):
+        block = hist[pick_ref[e]]
+        out_a[e] = jnp.where(live_ref[e] > 0, block, jnp.zeros_like(block))
+
     pl.semaphore_wait(enter.at[1], width - 1)
 
     @pl.loop(1, devices)
@@ -154,6 +162,27 @@
 
     in_a[me] = out_a[me]
     load_mixed.start()
+
+    spot = lax.broadcasted_iota(jnp.int32, (slots, slots), 0)
+    place = lax.broadcasted_iota(jnp.int32, (slots, slots), 1)
+    target = jnp.broadcast_to(target_ref[...], (slots, slots))
+    target_of = jnp.sum(jnp.where(spot == place, target, 0), axis=1, keepdims=True)
+    earlier = target * slots + place < target_of * slots + spot
+    rank = jnp.sum(earlier.astype(jnp.int32), axis=1, keepdims=True)
+    chosen = rank == place
+    order = jnp.sum(jnp.where(chosen, spot, 0), axis=0, keepdims=True)
+    ordered = jnp.sum(jnp.where(chosen, target_of, 0), axis=0, keepdims=True)
+    shifted = pltpu.roll(ordered, 1, 1)
+    same = jnp.where((shifted == ordered) & (place[0:1] > 0), 1, 0)
+    upto = jnp.sum((target_of <= place).astype(jnp.int32), axis=0, keepdims=True)
+    here = jnp.sum((target_of == place).astype(jnp.int32), axis=0, keepdims=True)
+    rank_rows[0:1] = order
+    rank_rows[1:2] = same
+    rank_rows[2:3] = jnp.maximum(upto - 1, 0)
+    rank_rows[3:4] = jnp.where(here > 0, 1, 0)
+    rank_rows[4:8] = jnp.zeros((4, rows), jnp.int32)
+    load_table = pltpu.make_async_copy(rank_rows, table, table_sem)
+    load_table.start()
 
     sources = (diag_hbm, next_hbm, prec_hbm)
 
@@ -230,46 +259,51 @@
                 device_id_type=MESH,
             )
 
-        red_src[phase, 0] = value
-        red_dom[phase, me_dom] = value
-
-        @pl.loop(1, doms)
-        def _(j):
-            dom_copy(lax.rem(me_dom + j, doms), me_dom).start()
-
-        @pl.loop(1, doms)
-        def _(j):
-            other = lax.rem(me_dom + j, doms)
-            dom_copy(other, other).wait_recv()
-
-        total = red_dom[phase, 0]
-        for j in range(1, doms):
-            total = total + red_dom[phase, j]
-        red_src[phase, 1] = total
-        red_sub[phase, me_sub] = total
-
-        @pl.loop(1, subs)
-        def _(j):
-            sub_copy(lax.rem(me_sub + j, subs), me_sub).start()
-
-        @pl.loop(1, subs)
-        def _(j):
-            other = lax.rem(me_sub + j, subs)
-            sub_copy(other, other).wait_recv()
-
-        total = red_sub[phase, 0]
-        for j in range(1, subs):
-            total = total + red_sub[phase, j]
-
-        @pl.loop(1, doms)
-        def _(j):
-            dom_copy(lax.rem(me_dom + j, doms), me_dom).wait_send()
-
-        @pl.loop(1, subs)
-        def _(j):
-            sub_copy(lax.rem(me_sub + j, subs), me_sub).wait_send()
-
-        return total
+        def begin():
+            red_src[phase, 0] = value
+            red_dom[phase, me_dom] = value
+
+            @pl.loop(1, doms)
+            def _(j):
+                dom_copy((me_dom + j) & (doms - 1), me_dom).start()
+
+        def middle_stage():
+            @pl.loop(1, doms)
+            def _(j):
+                other = (me_dom + j) & (doms - 1)
+                dom_copy(other, other).wait_recv()
+
+            total = red_dom[phase, 0]
+            for j in range(1, doms):
+                total = total + red_dom[phase, j]
+            red_src[phase, 1] = total
+            red_sub[phase, me_sub] = total
+
+            @pl.loop(1, subs)
+            def _(j):
+                sub_copy((me_sub + j) & (subs - 1), me_sub).start()
+
+        def finish():
+            @pl.loop(1, subs)
+            def _(j):
+                other = (me_sub + j) & (subs - 1)
+                sub_copy(other, other).wait_recv()
+
+            total = red_sub[phase, 0]
+            for j in range(1, subs):
+                total = total + red_sub[phase, j]
+
+            @pl.loop(1, doms)
+            def _(j):
+                dom_copy((me_dom + j) & (doms - 1), me_dom).wait_send()
+
+            @pl.loop(1, subs)
+            def _(j):
+                sub_copy((me_sub + j) & (subs - 1), me_sub).wait_send()
+
+            return total
+
+        return begin, middle_stage, finish
 
     link_copy = pltpu.make_async_remote_copy(
         src_ref=wa.at[count, pl.ds(2 * rows, rows)],
@@ -280,47 +314,74 @@
         device_id_type=MESH,
     )
     link_copy.start()
-    theta = reduce_over(0, trace[...])
-    theta = jnp.sum(jnp.sum(theta, axis=0, keepdims=True), axis=1, keepdims=True)
-    inv[...] = jnp.broadcast_to((1.0 * devices * count * rows) / theta, inv.shape)
+    begin, middle_stage, finish = reduce_over(0, trace[...])
+    begin()
+    load_table.wait()
 
     others = pl.ds(0, devices - 1)
     load_mixed.wait()
     pltpu.make_async_copy(in_a.at[others], in_a.at[others], a_recv).wait()
 
-    def mixed_tile(peer):
-        spot = relay_ref[peer]
-        return jnp.dot(in_a[spot], mixed[spot], preferred_element_type=F32)
+    def code_tiles(peers):
+        spots = [relay_ref[peer] for peer in peers]
+        values_of = [
+            jnp.dot(in_a[spot], mixed[spot], preferred_element_type=F32) for spot in spots
+        ]
+        tops = [jnp.max(jnp.abs(tile), axis=(0, 1), keepdims=True) for tile in values_of]
+        units = [jnp.where(top > 0.0, top, 1.0) / LEVELS for top in tops]
+        codes = [jnp.round(tile * (1.0 / unit)) for tile, unit in zip(values_of, units)]
+        for peer, code, unit in zip(peers, codes, units):
+            out_b[peer] = code.astype(jnp.int32).astype(jnp.int16)
+            unit_out[peer] = jnp.broadcast_to(unit, (1, rows))
 
     def send_tile(peer):
-        pltpu.make_async_remote_copy(
-            src_ref=out_b.at[peer],
-            dst_ref=tiles.at[me],
-            send_sem=b_send,
-            recv_sem=b_recv,
-            device_id=id_of(peer),
-            device_id_type=MESH,
-        ).start()
-
-    first = peer_of(1)
-    out_b[first] = mixed_tile(first)
-
-    def next_tile(s, ready):
-        peer = peer_of(s)
-        out_b[peer] = mixed_tile(peer)
-        send_tile(ready)
-        return peer
-
-    ready = lax.fori_loop(2, devices, next_tile, first)
-    tiles[me] = mixed_tile(me)
-    send_tile(ready)
+        for source, target, send, receive in (
+            (out_b, tiles, b_send, b_recv),
+            (unit_out, unit_in, c_send, c_recv),
+        ):
+            pltpu.make_async_remote_copy(
+                src_ref=source.at[peer],
+                dst_ref=target.at[me],
+                send_sem=send,
+                recv_sem=receive,
+                device_id=id_of(peer),
+                device_id_type=MESH,
+            ).start()
+
+    def group_of(i):
+        return tuple(peer_of(i * GROUP + 1 + j) for j in range(GROUP))
+
+    first = group_of(0)
+    code_tiles(first)
+
+    def next_tiles(i, ready):
+        peers = group_of(i)
+        code_tiles(peers)
+        for peer in ready:
+            send_tile(peer)
+        return peers
+
+    ready = lax.fori_loop(1, devices // GROUP, next_tiles, first)
+    tiles[me] = out_b[me]
+    unit_in[me] = unit_out[me]
+    for peer in ready[:-1]:
+        send_tile(peer)
+    middle_stage()
     pltpu.make_async_copy(out_a.at[others], out_a.at[others], a_send).wait()
     pltpu.make_async_copy(out_b.at[others], out_b.at[others], b_send).wait()
     pltpu.make_async_copy(tiles.at[others], tiles.at[others], b_recv).wait()
+    pltpu.make_async_copy(unit_out.at[others], unit_out.at[others], c_send).wait()
+    pltpu.make_async_copy(unit_in.at[others], unit_in.at[others], c_recv).wait()
+
+    theta = finish()
+    theta = jnp.sum(jnp.sum(theta, axis=0, keepdims=True), axis=1, keepdims=True)
+    inv[...] = jnp.broadcast_to((1.0 * devices * count * rows) / theta, inv.shape)
 
 
     def add_tile(j, running):
-        running = running * same_ref[j] + tiles[order_ref[j]]
+        spot = jnp.clip(table[0, j], 0, slots - 1)
+        tile = tiles[spot].astype(jnp.int32).astype(F32) * unit_in[spot]
+        running = running * table[1, j].astype(F32) + tile
         red[j] = running
         return running
 
@@ -328,7 +389,7 @@
 
     @pl.loop(0, count)
     def _(g):
-        res[0, g] = red[last_ref[g]] * have_ref[g]
+        res[0, g] = red[jnp.clip(table[2, g], 0, slots - 1)] * table[3, g].astype(F32)
 
     def precondition(blocks, k, fields):
         outs = [
@@ -367,22 +428,40 @@
             dots(6, [red[count + g] for g in blocks], laters)
             dots(7, fields, laters)
 
-    def inner(g, k):
-        near = [xs[k % 2, g + i] for i in range(4)]
+    def inner(g, k, width):
+        near = [xs[k % 2, g + i] for i in range(width + 2)]
         apply_blocks(
-            (g, g + 1), k, [jnp.concatenate([near[i + 1], near[i + 2], near[i]], axis=1) for i in range(2)]
+            tuple(g + i for i in range(width)),
+            k,
+            [
+                jnp.concatenate([near[i + 1], near[i + 2], near[i]], axis=1)
+                for i in range(width)
+            ],
         )
 
     def inners(start, stop, k):
-        @pl.loop(0, (stop - start) // 2)
+        whole = (stop - start) // BATCH
+
+        @pl.loop(0, whole)
         def _(i):
-            inner(start + 2 * i, k)
+            inner(start + BATCH * i, k, BATCH)
+
+        if (stop - start) % BATCH:
+            inner(start + BATCH * whole, k, (stop - start) % BATCH)
 
     def preconditions(start, stop):
-        @pl.loop(0, (stop - start) // 2)
+        whole = (stop - start) // BATCH
+
+        def some(g, width):
+            blocks = tuple(g + i for i in range(width))
+            precondition(blocks, 0, [res[0, block] for block in blocks])
+
+        @pl.loop(0, whole)
         def _(i):
-            g = start + 2 * i
-            precondition((g, g + 1), 0, (res[0, g], res[0, g + 1]))
+            some(start + BATCH * i, BATCH)
+
+        if (stop - start) % BATCH:
+            some(start + BATCH * whole, (stop - start) % BATCH)
 
     def halo_copy(k, side):
         return pltpu.make_async_remote_copy(
@@ -428,7 +507,10 @@
     for j in range(8):
         packed = packed + jnp.where(lane == j, jnp.sum(acc[j], axis=1, keepdims=True), 0.0)
     packed = jnp.concatenate([packed, jnp.zeros((rows - values, rows), F32)], axis=0)
-    total = reduce_over(1, packed.T[0:8])
+    begin, middle_stage, finish = reduce_over(1, packed.T[0:8])
+    begin()
+    middle_stage()
+    total = finish()
 
     def over(top, bottom):
         usable = bottom != 0.0
@@ -468,7 +550,7 @@
     put_r.wait()
 
 
-def mass_solve(order, same, last, have, links, pick, live, relay, history, mixed, mass_diag, mass_next, precond):
+def mass_solve(target, links, pick, live, relay, history, mixed, mass_diag, mass_next, precond):
     doms, subs = lax.axis_size("dom"), lax.axis_size("sub")
     slots = mixed.shape[0]
     blocks, values, rows = history.shape
@@ -485,15 +567,17 @@
     return pl.pallas_call(
         kernel,
         out_shape=(field, field),
-        in_specs=[smem] * 8 + [hbm] * 5,
+        in_specs=[pl.BlockSpec(memory_space=pltpu.VMEM)] + [smem] * 4 + [hbm] * 5,
         out_specs=(hbm, hbm),
         scratch_shapes=[
             pltpu.VMEM((blocks, values, rows), BF16),
             pltpu.VMEM((slots, rows, rows), BF16),
             pltpu.VMEM((slots, values, rows), BF16),
             pltpu.VMEM((slots, values, rows), BF16),
-            pltpu.VMEM((slots, values, rows), F32),
-            pltpu.VMEM((slots, values, rows), F32),
+            pltpu.VMEM((slots, values, rows), jnp.int16),
+            pltpu.VMEM((slots, values, rows), jnp.int16),
+            pltpu.VMEM((slots, 1, rows), F32),
+            pltpu.VMEM((slots, 1, rows), F32),
             pltpu.VMEM((2, 3, CHUNK, rows, rows), F32),
             pltpu.VMEM((count + 1, 3 * rows, 2 * rows), BF16),
             pltpu.VMEM((count, rows, 2 * rows), BF16),
@@ -509,7 +593,12 @@
             pltpu.VMEM((2, 2, 8, rows), F32),
             pltpu.VMEM((2, doms, 8, rows), F32),
             pltpu.VMEM((2, subs, 8, rows), F32),
+            pltpu.VMEM((8, rows), jnp.int32),
+            pltpu.SMEM((8, rows), jnp.int32),
+            dma,
             pltpu.SemaphoreType.REGULAR((2,)),
+            dma,
+            dma,
             dma,
             dma,
             dma,
@@ -530,22 +619,7 @@
         compiler_params=pltpu.CompilerParams(
             collective_id=0, has_side_effects=True, vmem_limit_bytes=60 * 1024 * 1024
         ),
-    )(order, same, last, have, links, pick, live, relay, history, mixed, mass_diag, mass_next, precond)
-
-
-def target_order(targets, count):
-    slots = targets.shape[0]
-    spot = jnp.arange(slots, dtype=jnp.int32)
-    key = targets * slots + spot
-    rank = jnp.sum((key[None, :] < key[:, None]).astype(jnp.int32), axis=1)
-    at = rank[None, :] == spot[:, None]
-    order = jnp.sum(jnp.where(at, spot[None, :], 0), axis=1)
-    ordered = jnp.sum(jnp.where(at, targets[None, :], 0), axis=1)
-    same = jnp.concatenate([jnp.zeros((1,), F32), (ordered[1:] == ordered[:-1]).astype(F32)])
-    block = jnp.arange(count, dtype=jnp.int32)
-    upto = jnp.sum((targets[None, :] <= block[:, None]).astype(jnp.int32), axis=1)
-    have = jnp.any(targets[None, :] == block[:, None], axis=1).astype(F32)
-    return order, same, jnp.maximum(upto - 1, 0), have
+    )(target, links, pick, live, relay, history, mixed, mass_diag, mass_next, precond)
 
 
 def body(
@@ -560,14 +634,8 @@
     coupling,
     precond,
 ):
-    new_count = mass_diag.shape[0]
-    targets = relay_target.reshape(-1)
-    order, same, last, have = target_order(targets, new_count)
     return mass_solve(
-        order,
-        same,
-        last,
-        have,
+        relay_target.reshape(1, -1),
         coupling,
         send_list.reshape(-1),
         send_count.reshape(-1),

time: 157 us -> 106 us (0.68)
  Pallas kernels: 146 us -> 100 us
  other arithmetic: 5.4 us -> 0 us
    pallas_call x1, Pallas kernels: 146 us -> 100 us  [mass_solve(): pl.pallas_call(kernel, out_shape=(field, field), in_specs=[pl.BlockSpec(m...]
    reduce_sum x3 -> x0, other arithmetic: 2.22 us -> none  [the longest x1 1.29 us: target_order(): ordered = jnp.sum(jnp.where(at, targets[None, :], 0), axis=1)]
where the time goes in v4:
time: 106 us; the launch traced here: 105 us
  Pallas kernels  100 us (94%)
  local copies, waits for them, and re-layouts  4.63 us (4%)
    pallas_call x1, Pallas kernels, mass_solve(): pl.pallas_call(kernel, out_shape=(field, field), in_specs=[pl.BlockSpec(m...  100 us
    unnamed x4, local copies, waits for them, and re-layouts  4.63 us

profile of v4, /device:TPU:1, one launch (start us, length us, event | category | flops | bytes accessed | tf_op | source)
XLA Modules:
  0.0 105.3 jit_solution(2933047225627024688)
XLA Ops:
  0.6 100.0 %shard_map.113 = (f32[64,64,128]{2,1,0:T(8,128)}, f32[64,64,128]{2,1,0:T(8,128)}) custom-call(s32[1,128]{1,0:T(1,128)} %bitcast.4, s32[64]{0:T(128)} %refs_1_.1, s32[128]{0:T(128)} %bitcast.5, s32[128]{0:T(128)} %bitcast.6, s32[128]{0:T(128)} %bitcast.7, bf16[32,64,128]{2,1,0:T(8,128)(2,1)} %refs_5_.1, bf16[128,128,128]{2,1,0:T(8,128)(2,1)} %refs_6_.1, ...), custom_call_target="tpu_custom_call" | custom-call | tf_op jit(solution)/shard_map/pallas_call | solution.py:567
  100.6 0.0 copy-start
  100.6 3.3 %copy.14 = f32[64,64,128]{2,1,0:T(8,128)} copy(f32[64,64,128]{2,1,0:T(8,128)} %get-tuple-element.4) | data formatting | bytes 4194304
  103.9 0.0 copy-done
  103.9 1.3 %copy.15 = f32[64,64,128]{2,1,0:T(8,128)} copy(f32[64,64,128]{2,1,0:T(8,128)S(1)} %copy-done) | data formatting | bytes 4194304
Async XLA Ops:
  100.6 3.3 %copy-start = (f32[64,64,128]{2,1,0:T(8,128)S(1)}, f32[64,64,128]{2,1,0:T(8,128)}, u32[]{:S(2)}) copy-start(f32[64,64,128]{2,1,0:T(8,128)} %get-tuple-element.5) | copy-start | bytes 6291460

commit v5 on v4

--- a/solution.py
+++ b/solution.py
@@ -12,6 +12,9 @@
 CHUNK = 4
 ORDER = 37
 GROUP = 4
+PIECE = 8
+LIMIT1 = 46000
+LIMIT2 = 8000
 BATCH = 8
 LEVELS = 32767.0
 FIRST_BITS = 0b0101010
@@ -46,8 +49,9 @@
     diag_hbm,
     next_hbm,
     prec_hbm,
-    x_hbm,
-    res_hbm,
+    res,
+    red,
+    mix_ref,
     hist,
     mixed,
     out_a,
@@ -61,8 +65,6 @@
     wp,
     diag_a,
     diag_p,
-    res,
-    red,
     xs,
     halo,
     acc,
@@ -92,7 +94,6 @@
     dom_recv,
     sub_send,
     sub_recv,
-    out_sem,
 ):
     doms, subs, count, values, rows, slots = shape
     devices = doms * subs
@@ -533,21 +534,40 @@
     e1 = jnp.broadcast_to(weights[0:values, 1:2], (values, rows))
     e2 = jnp.broadcast_to(weights[0:values, 2:3], (values, rows))
     scale = inv[0:1]
-    x0, x1, x2 = (1.0 - e0) * scale, (1.0 - e1) * scale, (1.0 - e2) * scale
-    r1, r2, r3 = e1 - e0, e2 - e1, 1.0 - e2
-
-    @pl.loop(0, count)
-    def _(g):
-        u0, u1, u2 = red[g], red[count + g], red[2 * count + g]
-        red[g] = x0 * u0 + x1 * u1 + x2 * u2
-        res[0, g] = e0 * res[0, g] + r1 * res[1, g] + r2 * res[2, g] + r3 * res[3, g]
-
-    put_x = pltpu.make_async_copy(red.at[pl.ds(0, count)], x_hbm, out_sem.at[0])
-    put_r = pltpu.make_async_copy(res.at[0], res_hbm, out_sem.at[1])
-    put_x.start()
-    put_r.start()
-    put_x.wait()
-    put_r.wait()
+    for j, factor in enumerate(
+        ((1.0 - e0) * scale, (1.0 - e1) * scale, (1.0 - e2) * scale, e0, e1 - e0, e2 - e1, 1.0 - e2)
+    ):
+        mix_ref[j] = factor
+
+
+def combine_kernel(res, red, mix_ref, x_hbm, res_hbm, x_all, r_all, sems):
+    count, values, rows = x_all.shape
+    x0, x1, x2, r0, r1, r2, r3 = (mix_ref[j] for j in range(7))
+    pieces = count // PIECE
+
+    def puts(piece):
+        part = pl.ds(piece * PIECE, PIECE)
+        return (
+            pltpu.make_async_copy(x_all.at[part], x_hbm.at[part], sems.at[0, piece]),
+            pltpu.make_async_copy(r_all.at[part], res_hbm.at[part], sems.at[1, piece]),
+        )
+
+    @pl.loop(0, pieces)
+    def _(piece):
+        @pl.loop(0, PIECE // 2)
+        def _(i):
+            for j in range(2):
+                g = piece * PIECE + 2 * i + j
+                x_all[g] = x0 * red[g] + x1 * red[count + g] + x2 * red[2 * count + g]
+                r_all[g] = r0 * res[0, g] + r1 * res[1, g] + r2 * res[2, g] + r3 * res[3, g]
+
+        for put in puts(piece):
+            put.start()
+
+    @pl.loop(0, pieces)
+    def _(piece):
+        for put in puts(piece):
+            put.wait()
 
 
 def mass_solve(target, links, pick, live, relay, history, mixed, mass_diag, mass_next, precond):
@@ -564,11 +584,17 @@
     hbm = pl.BlockSpec(memory_space=pl.ANY)
     field = jax.ShapeDtypeStruct((count, values, rows), F32)
     dma = pltpu.SemaphoreType.DMA
-    return pl.pallas_call(
+    vmem = pl.BlockSpec(memory_space=pltpu.VMEM)
+    parts = (
+        pltpu.VMEM((STEPS + 1, count, values, rows), F32),
+        pltpu.VMEM((STEPS * count, values, rows), F32),
+        pltpu.VMEM((7, values, rows), F32),
+    )
+    parts = pl.pallas_call(
         kernel,
-        out_shape=(field, field),
+        out_shape=parts,
         in_specs=[pl.BlockSpec(memory_space=pltpu.VMEM)] + [smem] * 4 + [hbm] * 5,
-        out_specs=(hbm, hbm),
+        out_specs=(vmem,) * 3,
         scratch_shapes=[
             pltpu.VMEM((blocks, values, rows), BF16),
             pltpu.VMEM((slots, rows, rows), BF16),
@@ -583,8 +609,6 @@
             pltpu.VMEM((count, rows, 2 * rows), BF16),
             pltpu.VMEM((count, 1, rows), F32),
             pltpu.VMEM((count, 1, rows), F32),
-            pltpu.VMEM((STEPS + 1, count, values, rows), F32),
-            pltpu.VMEM((STEPS * count, values, rows), F32),
             pltpu.VMEM((2, count + 2, 2 * values, rows), BF16),
             pltpu.VMEM((STEPS, 2, 2 * values, rows), BF16),
             pltpu.VMEM((8, values, rows), F32),
@@ -614,12 +638,23 @@
             dma((2, doms)),
             dma((2, subs)),
             dma((2, subs)),
-            dma((2,)),
         ],
         compiler_params=pltpu.CompilerParams(
-            collective_id=0, has_side_effects=True, vmem_limit_bytes=60 * 1024 * 1024
+            collective_id=0, has_side_effects=True, vmem_limit_bytes=LIMIT1 * 1024
         ),
     )(target, links, pick, live, relay, history, mixed, mass_diag, mass_next, precond)
+    return pl.pallas_call(
+        combine_kernel,
+        out_shape=(field, field),
+        in_specs=[vmem] * 3,
+        out_specs=(hbm, hbm),
+        scratch_shapes=[
+            pltpu.VMEM((count, values, rows), F32),
+            pltpu.VMEM((count, values, rows), F32),
+            dma((2, count // PIECE)),
+        ],
+        compiler_params=pltpu.CompilerParams(vmem_limit_bytes=LIMIT2 * 1024),
+    )(*parts)
 
 
 def body(

time: 106 us -> 99.9 us (0.942)
  local copies, waits for them, and re-layouts: 4.63 us -> 0 us
  Pallas kernels: 100 us -> 98.9 us
    unnamed x4 -> x0, local copies, waits for them, and re-layouts: 4.63 us -> none
    pallas_call x1 -> x2, Pallas kernels: 100 us -> 98.9 us  [the longest x1 96.6 us: mass_solve(): pl.pallas_call(kernel, out_shape=parts, in_specs=[pl.BlockSpec(memory_spa...]
where the time goes in v5:
time: 99.9 us; the launch traced here: 99.5 us
  Pallas kernels  98.9 us (99%)
    pallas_call x1, Pallas kernels, mass_solve(): pl.pallas_call(kernel, out_shape=parts, in_specs=[pl.BlockSpec(memory_spa...  96.6 us
    pallas_call x1, Pallas kernels, mass_solve(): pl.pallas_call(combine_kernel, out_shape=(field, field), in_specs=[vmem]...  2.28 us

profile of v5, /device:TPU:1, one launch (start us, length us, event | category | flops | bytes accessed | tf_op | source)
XLA Modules:
  0.0 99.5 jit_solution(2794327944664404828)
XLA Ops:
  0.6 96.6 %shard_map.113 = (f32[4,64,64,128]{3,2,1,0:T(8,128)S(1)}, f32[192,64,128]{2,1,0:T(8,128)S(1)}, f32[7,64,128]{2,1,0:T(8,128)S(1)}) custom-call(s32[1,128]{1,0:T(1,128)} %bitcast.4, s32[64]{0:T(128)} %refs_1_.1, s32[128]{0:T(128)} %bitcast.5, s32[128]{0:T(128)} %bitcast.6, s32[128]{0:T(128)} %bitcast.7, bf16[32,64,128]{2,1,0:T(8,128)(2,1)} %refs_5_.1, ...), custom_call_target="tpu_custom_call" | custom-call | tf_op jit(solution)/shard_map/pallas_call | solution.py:593
  97.2 2.3 %shard_map.114 = (f32[64,64,128]{2,1,0:T(8,128)}, f32[64,64,128]{2,1,0:T(8,128)}) custom-call(f32[4,64,64,128]{3,2,1,0:T(8,128)S(1)} %get-tuple-element.5.res, f32[192,64,128]{2,1,0:T(8,128)S(1)} %get-tuple-element.6.red, f32[7,64,128]{2,1,0:T(8,128)S(1)} %get-tuple-element.7.mix_ref), custom_call_target="tpu_custom_call" | custom-call | tf_op jit(solution)/shard_map/pallas_call | solution.py:646

commit v6 on v5

--- a/solution.py
+++ b/solution.py
@@ -12,6 +12,8 @@
 CHUNK = 4
 ORDER = 37
 GROUP = 4
+PARTS = 2
+SMALLEST = 1e-30
 PIECE = 8
 LIMIT1 = 46000
 LIMIT2 = 8000
@@ -55,11 +57,14 @@
     hist,
     mixed,
     out_a,
-    in_a,
+    in_a_0,
+    in_a_1,
     out_b,
-    tiles,
+    tiles_0,
+    tiles_1,
     unit_out,
-    unit_in,
+    unit_in_0,
+    unit_in_1,
     stage,
     wa,
     wp,
@@ -97,6 +102,8 @@
 ):
     doms, subs, count, values, rows, slots = shape
     devices = doms * subs
+    part = values // PARTS
+    in_a, tiles, unit_in = (in_a_0, in_a_1), (tiles_0, tiles_1), (unit_in_0, unit_in_1)
     me_dom, me_sub = lax.axis_index("dom"), lax.axis_index("sub")
     me = me_dom * subs + me_sub
     after = lax.rem(me + 1, devices)
@@ -145,23 +152,28 @@
     @pl.loop(0, devices)
     def _(e):
         block = hist[pick_ref[e]]
-        out_a[e] = jnp.where(live_ref[e] > 0, block, jnp.zeros_like(block))
+        block = jnp.where(live_ref[e] > 0, block, jnp.zeros_like(block))
+        for h in range(PARTS):
+            out_a[h, e] = block[h * part : (h + 1) * part]
 
     pl.semaphore_wait(enter.at[1], width - 1)
 
-    @pl.loop(1, devices)
-    def _(s):
-        peer = peer_of(s)
-        pltpu.make_async_remote_copy(
-            src_ref=out_a.at[peer],
-            dst_ref=in_a.at[me],
-            send_sem=a_send,
-            recv_sem=a_recv,
-            device_id=id_of(peer),
-            device_id_type=MESH,
-        ).start()
-
-    in_a[me] = out_a[me]
+    for h in range(PARTS):
+
+        @pl.loop(1, devices)
+        def _(s):
+            peer = peer_of(s)
+            pltpu.make_async_remote_copy(
+                src_ref=out_a.at[h, peer],
+                dst_ref=in_a[h].at[me],
+                send_sem=a_send.at[h],
+                recv_sem=a_recv.at[h],
+                device_id=id_of(peer),
+                device_id_type=MESH,
+            ).start()
+
+    for h in range(PARTS):
+        in_a[h][me] = out_a[h, me]
     load_mixed.start()
 
     spot = lax.broadcasted_iota(jnp.int32, (slots, slots), 0)
@@ -321,30 +333,33 @@
 
     others = pl.ds(0, devices - 1)
     load_mixed.wait()
-    pltpu.make_async_copy(in_a.at[others], in_a.at[others], a_recv).wait()
-
-    def code_tiles(peers):
+
+    def wait_all(buffer, h, semaphore):
+        view = buffer.at[others]
+        pltpu.make_async_copy(view, view, semaphore.at[h]).wait()
+
+    def code_tiles(h, peers):
         spots = [relay_ref[peer] for peer in peers]
         values_of = [
-            jnp.dot(in_a[spot], mixed[spot], preferred_element_type=F32) for spot in spots
+            jnp.dot(in_a[h][spot], mixed[spot], preferred_element_type=F32) for spot in spots
         ]
         tops = [jnp.max(jnp.abs(tile), axis=(0, 1), keepdims=True) for tile in values_of]
-        units = [jnp.where(top > 0.0, top, 1.0) / LEVELS for top in tops]
+        units = [jnp.maximum(top, SMALLEST) / LEVELS for top in tops]
         codes = [jnp.round(tile * (1.0 / unit)) for tile, unit in zip(values_of, units)]
         for peer, code, unit in zip(peers, codes, units):
-            out_b[peer] = code.astype(jnp.int32).astype(jnp.int16)
-            unit_out[peer] = jnp.broadcast_to(unit, (1, rows))
-
-    def send_tile(peer):
+            out_b[h, peer] = code.astype(jnp.int32).astype(jnp.int16)
+            unit_out[h, peer] = jnp.broadcast_to(unit, (1, rows))
+
+    def send_tile(h, peer):
         for source, target, send, receive in (
             (out_b, tiles, b_send, b_recv),
             (unit_out, unit_in, c_send, c_recv),
         ):
             pltpu.make_async_remote_copy(
-                src_ref=source.at[peer],
-                dst_ref=target.at[me],
-                send_sem=send,
-                recv_sem=receive,
+                src_ref=source.at[h, peer],
+                dst_ref=target[h].at[me],
+                send_sem=send.at[h],
+                recv_sem=receive.at[h],
                 device_id=id_of(peer),
                 device_id_type=MESH,
             ).start()
@@ -352,45 +367,65 @@
     def group_of(i):
         return tuple(peer_of(i * GROUP + 1 + j) for j in range(GROUP))
 
-    first = group_of(0)
-    code_tiles(first)
-
-    def next_tiles(i, ready):
-        peers = group_of(i)
-        code_tiles(peers)
-        for peer in ready:
-            send_tile(peer)
-        return peers
-
-    ready = lax.fori_loop(1, devices // GROUP, next_tiles, first)
-    tiles[me] = out_b[me]
-    unit_in[me] = unit_out[me]
-    for peer in ready[:-1]:
-        send_tile(peer)
-    middle_stage()
-    pltpu.make_async_copy(out_a.at[others], out_a.at[others], a_send).wait()
-    pltpu.make_async_copy(out_b.at[others], out_b.at[others], b_send).wait()
-    pltpu.make_async_copy(tiles.at[others], tiles.at[others], b_recv).wait()
-    pltpu.make_async_copy(unit_out.at[others], unit_out.at[others], c_send).wait()
-    pltpu.make_async_copy(unit_in.at[others], unit_in.at[others], c_recv).wait()
+    def code_part(h):
+        def step(i, ready):
+            peers = group_of(i)
+            code_tiles(h, peers)
+            for peer in ready:
+                send_tile(h, peer)
+            return peers
+
+        first = group_of(0)
+        code_tiles(h, first)
+        ready = lax.fori_loop(1, devices // GROUP, step, first)
+        tiles[h][me] = out_b[h, me]
+        unit_in[h][me] = unit_out[h, me]
+        for peer in ready[:-1]:
+            send_tile(h, peer)
+
+    for h in range(PARTS):
+        wait_all(in_a[h], h, a_recv)
+        if h == PARTS - 1:
+            middle_stage()
+        code_part(h)
+    for h in range(PARTS):
+        wait_all(out_a.at[h], h, a_send)
+
+    def arrived(h):
+        wait_all(out_b.at[h], h, b_send)
+        wait_all(tiles[h], h, b_recv)
+        wait_all(unit_out.at[h], h, c_send)
+        wait_all(unit_in[h], h, c_recv)
+
+    def right_hand_side(h):
+        rows_of = pl.ds(h * part, part)
+
+        def add_tiles(i, running):
+            places = [i * GROUP + j for j in range(GROUP)]
+            spots = [jnp.clip(table[0, j], 0, slots - 1) for j in places]
+            terms = [
+                tiles[h][spot].astype(jnp.int32).astype(F32) * unit_in[h][spot] for spot in spots
+            ]
+            for j, term in zip(places, terms):
+                running = running * table[1, j].astype(F32) + term
+                red[j, rows_of] = running
+            return running
+
+        lax.fori_loop(0, slots // GROUP, add_tiles, jnp.zeros((part, rows), F32))
+
+        @pl.loop(0, count // 2)
+        def _(i):
+            for g in (2 * i, 2 * i + 1):
+                last = jnp.clip(table[2, g], 0, slots - 1)
+                res[0, g, rows_of] = red[last, rows_of] * table[3, g].astype(F32)
+
+    for h in range(PARTS):
+        arrived(h)
+        right_hand_side(h)
 
     theta = finish()
     theta = jnp.sum(jnp.sum(theta, axis=0, keepdims=True), axis=1, keepdims=True)
     inv[...] = jnp.broadcast_to((1.0 * devices * count * rows) / theta, inv.shape)
-
-
-    def add_tile(j, running):
-        spot = jnp.clip(table[0, j], 0, slots - 1)
-        tile = tiles[spot].astype(jnp.int32).astype(F32) * unit_in[spot]
-        running = running * table[1, j].astype(F32) + tile
-        red[j] = running
-        return running
-
-    lax.fori_loop(0, slots, add_tile, jnp.zeros((values, rows), F32))
-
-    @pl.loop(0, count)
-    def _(g):
-        res[0, g] = red[jnp.clip(table[2, g], 0, slots - 1)] * table[3, g].astype(F32)
 
     def precondition(blocks, k, fields):
         outs = [
@@ -598,10 +633,13 @@
         scratch_shapes=[
             pltpu.VMEM((blocks, values, rows), BF16),
             pltpu.VMEM((slots, rows, rows), BF16),
-            pltpu.VMEM((slots, values, rows), BF16),
-            pltpu.VMEM((slots, values, rows), BF16),
-            pltpu.VMEM((slots, values, rows), jnp.int16),
-            pltpu.VMEM((slots, values, rows), jnp.int16),
+            pltpu.VMEM((PARTS, slots, values // PARTS, rows), BF16),
+            pltpu.VMEM((slots, values // PARTS, rows), BF16),
+            pltpu.VMEM((slots, values // PARTS, rows), BF16),
+            pltpu.VMEM((PARTS, slots, values // PARTS, rows), jnp.int16),
+            pltpu.VMEM((slots, values // PARTS, rows), jnp.int16),
+            pltpu.VMEM((slots, values // PARTS, rows), jnp.int16),
+            pltpu.VMEM((PARTS, slots, 1, rows), F32),
             pltpu.VMEM((slots, 1, rows), F32),
             pltpu.VMEM((slots, 1, rows), F32),
             pltpu.VMEM((2, 3, CHUNK, rows, rows), F32),
@@ -623,12 +661,12 @@
             pltpu.SemaphoreType.REGULAR((2,)),
             dma,
             dma,
-            dma,
-            dma,
-            dma,
-            dma,
-            dma,
-            dma,
+            dma((PARTS,)),
+            dma((PARTS,)),
+            dma((PARTS,)),
+            dma((PARTS,)),
+            dma((PARTS,)),
+            dma((PARTS,)),
             dma((2, 3)),
             dma((STEPS, 2)),
             dma((STEPS, 2)),

time: 99.9 us -> 95 us (0.951)
  Pallas kernels: 98.9 us -> 94 us
    pallas_call x1, Pallas kernels: 96.6 us -> 91.7 us  [mass_solve(): pl.pallas_call(kernel, out_shape=parts, in_specs=[pl.BlockSpec(memory_spa...]
where the time goes in v6:
time: 95 us; the launch traced here: 94.6 us
  Pallas kernels  94 us (99%)
    pallas_call x1, Pallas kernels, mass_solve(): pl.pallas_call(kernel, out_shape=parts, in_specs=[pl.BlockSpec(memory_spa...  91.7 us
    pallas_call x1, Pallas kernels, mass_solve(): pl.pallas_call(combine_kernel, out_shape=(field, field), in_specs=[vmem]...  2.28 us

profile of v6, /device:TPU:1, one launch (start us, length us, event | category | flops | bytes accessed | tf_op | source)
XLA Modules:
  0.0 94.6 jit_solution(12418851942273504319)
XLA Ops:
  0.6 91.7 %shard_map.113 = (f32[4,64,64,128]{3,2,1,0:T(8,128)S(1)}, f32[192,64,128]{2,1,0:T(8,128)S(1)}, f32[7,64,128]{2,1,0:T(8,128)S(1)}) custom-call(s32[1,128]{1,0:T(1,128)} %bitcast.4, s32[64]{0:T(128)} %refs_1_.1, s32[128]{0:T(128)} %bitcast.5, s32[128]{0:T(128)} %bitcast.6, s32[128]{0:T(128)} %bitcast.7, bf16[32,64,128]{2,1,0:T(8,128)(2,1)} %refs_5_.1, ...), custom_call_target="tpu_custom_call" | custom-call | tf_op jit(solution)/shard_map/pallas_call | solution.py:628
  92.3 2.3 %shard_map.114 = (f32[64,64,128]{2,1,0:T(8,128)}, f32[64,64,128]{2,1,0:T(8,128)}) custom-call(f32[4,64,64,128]{3,2,1,0:T(8,128)S(1)} %get-tuple-element.5.res, f32[192,64,128]{2,1,0:T(8,128)S(1)} %get-tuple-element.6.red, f32[7,64,128]{2,1,0:T(8,128)S(1)} %get-tuple-element.7.mix_ref), custom_call_target="tpu_custom_call" | custom-call | tf_op jit(solution)/shard_map/pallas_call | solution.py:684

commit v7 on v6

--- a/solution.py
+++ b/solution.py
@@ -11,10 +11,11 @@
 STEPS = 3
 CHUNK = 4
 ORDER = 37
-GROUP = 4
+GROUP = 8
 PARTS = 2
 SMALLEST = 1e-30
 PIECE = 8
+SUBLANES = 8
 LIMIT1 = 46000
 LIMIT2 = 8000
 BATCH = 8
@@ -276,13 +277,11 @@
             red_src[phase, 0] = value
             red_dom[phase, me_dom] = value
 
-            @pl.loop(1, doms)
-            def _(j):
+            for j in range(1, doms):
                 dom_copy((me_dom + j) & (doms - 1), me_dom).start()
 
         def middle_stage():
-            @pl.loop(1, doms)
-            def _(j):
+            for j in range(1, doms):
                 other = (me_dom + j) & (doms - 1)
                 dom_copy(other, other).wait_recv()
 
@@ -292,13 +291,11 @@
             red_src[phase, 1] = total
             red_sub[phase, me_sub] = total
 
-            @pl.loop(1, subs)
-            def _(j):
+            for j in range(1, subs):
                 sub_copy((me_sub + j) & (subs - 1), me_sub).start()
 
         def finish():
-            @pl.loop(1, subs)
-            def _(j):
+            for j in range(1, subs):
                 other = (me_sub + j) & (subs - 1)
                 sub_copy(other, other).wait_recv()
 
@@ -306,12 +303,10 @@
             for j in range(1, subs):
                 total = total + red_sub[phase, j]
 
-            @pl.loop(1, doms)
-            def _(j):
+            for j in range(1, doms):
                 dom_copy((me_dom + j) & (doms - 1), me_dom).wait_send()
 
-            @pl.loop(1, subs)
-            def _(j):
+            for j in range(1, subs):
                 sub_copy((me_sub + j) & (subs - 1), me_sub).wait_send()
 
             return total
@@ -577,7 +572,6 @@
 
 def combine_kernel(res, red, mix_ref, x_hbm, res_hbm, x_all, r_all, sems):
     count, values, rows = x_all.shape
-    x0, x1, x2, r0, r1, r2, r3 = (mix_ref[j] for j in range(7))
     pieces = count // PIECE
 
     def puts(piece):
@@ -589,12 +583,20 @@
 
     @pl.loop(0, pieces)
     def _(piece):
-        @pl.loop(0, PIECE // 2)
-        def _(i):
-            for j in range(2):
-                g = piece * PIECE + 2 * i + j
-                x_all[g] = x0 * red[g] + x1 * red[count + g] + x2 * red[2 * count + g]
-                r_all[g] = r0 * res[0, g] + r1 * res[1, g] + r2 * res[2, g] + r3 * res[3, g]
+        for top in range(0, values, SUBLANES):
+            some = pl.ds(top, SUBLANES)
+            x0, x1, x2, r0, r1, r2, r3 = (mix_ref[j, some] for j in range(7))
+            for i in range(PIECE):
+                g = piece * PIECE + i
+                x_all[g, some] = (
+                    x0 * red[g, some] + x1 * red[count + g, some] + x2 * red[2 * count + g, some]
+                )
+                r_all[g, some] = (
+                    r0 * res[0, g, some]
+                    + r1 * res[1, g, some]
+                    + r2 * res[2, g, some]
+                    + r3 * res[3, g, some]
+                )
 
         for put in puts(piece):
             put.start()

time: 95 us -> 94.4 us (level)
  no operation moved by 1% of the time
where the time goes in v7:
time: 94.4 us; the launch traced here: 94 us
  Pallas kernels  93.4 us (99%)
    pallas_call x1, Pallas kernels, mass_solve(): pl.pallas_call(kernel, out_shape=parts, in_specs=[pl.BlockSpec(memory_spa...  91.2 us
    pallas_call x1, Pallas kernels, mass_solve(): pl.pallas_call(combine_kernel, out_shape=(field, field), in_specs=[vmem]...  2.19 us

profile of v7, /device:TPU:1, one launch (start us, length us, event | category | flops | bytes accessed | tf_op | source)
XLA Modules:
  0.0 94.0 jit_solution(12544434988327012097)
XLA Ops:
  0.6 91.2 %shard_map.113 = (f32[4,64,64,128]{3,2,1,0:T(8,128)S(1)}, f32[192,64,128]{2,1,0:T(8,128)S(1)}, f32[7,64,128]{2,1,0:T(8,128)S(1)}) custom-call(s32[1,128]{1,0:T(1,128)} %bitcast.4, s32[64]{0:T(128)} %refs_1_.1, s32[128]{0:T(128)} %bitcast.5, s32[128]{0:T(128)} %bitcast.6, s32[128]{0:T(128)} %bitcast.7, bf16[32,64,128]{2,1,0:T(8,128)(2,1)} %refs_5_.1, ...), custom_call_target="tpu_custom_call" | custom-call | tf_op jit(solution)/shard_map/pallas_call | solution.py:630
  91.8 2.2 %shard_map.114 = (f32[64,64,128]{2,1,0:T(8,128)}, f32[64,64,128]{2,1,0:T(8,128)}) custom-call(f32[4,64,64,128]{3,2,1,0:T(8,128)S(1)} %get-tuple-element.5.res, f32[192,64,128]{2,1,0:T(8,128)S(1)} %get-tuple-element.6.red, f32[7,64,128]{2,1,0:T(8,128)S(1)} %get-tuple-element.7.mix_ref), custom_call_target="tpu_custom_call" | custom-call | tf_op jit(solution)/shard_map/pallas_call | solution.py:686

commit v8 on v7

--- a/solution.py
+++ b/solution.py
@@ -18,7 +18,7 @@
 SUBLANES = 8
 LIMIT1 = 46000
 LIMIT2 = 8000
-BATCH = 8
+BATCH = 16
 LEVELS = 32767.0
 FIRST_BITS = 0b0101010
 

time: 94.4 us -> 93.8 us (level)
  no operation moved by 1% of the time
where the time goes in v8:
time: 93.8 us; the launch traced here: 93.4 us
  Pallas kernels  92.8 us (99%)
    pallas_call x1, Pallas kernels, mass_solve(): pl.pallas_call(kernel, out_shape=parts, in_specs=[pl.BlockSpec(memory_spa...  90.6 us
    pallas_call x1, Pallas kernels, mass_solve(): pl.pallas_call(combine_kernel, out_shape=(field, field), in_specs=[vmem]...  2.19 us

profile of v8, /device:TPU:1, one launch (start us, length us, event | category | flops | bytes accessed | tf_op | source)
XLA Modules:
  0.0 93.4 jit_solution(12064461310049536407)
XLA Ops:
  0.6 90.6 %shard_map.113 = (f32[4,64,64,128]{3,2,1,0:T(8,128)S(1)}, f32[192,64,128]{2,1,0:T(8,128)S(1)}, f32[7,64,128]{2,1,0:T(8,128)S(1)}) custom-call(s32[1,128]{1,0:T(1,128)} %bitcast.4, s32[64]{0:T(128)} %refs_1_.1, s32[128]{0:T(128)} %bitcast.5, s32[128]{0:T(128)} %bitcast.6, s32[128]{0:T(128)} %bitcast.7, bf16[32,64,128]{2,1,0:T(8,128)(2,1)} %refs_5_.1, ...), custom_call_target="tpu_custom_call" | custom-call | tf_op jit(solution)/shard_map/pallas_call | solution.py:630
  91.2 2.2 %shard_map.114 = (f32[64,64,128]{2,1,0:T(8,128)}, f32[64,64,128]{2,1,0:T(8,128)}) custom-call(f32[4,64,64,128]{3,2,1,0:T(8,128)S(1)} %get-tuple-element.5.res, f32[192,64,128]{2,1,0:T(8,128)S(1)} %get-tuple-element.6.red, f32[7,64,128]{2,1,0:T(8,128)S(1)} %get-tuple-element.7.mix_ref), custom_call_target="tpu_custom_call" | custom-call | tf_op jit(solution)/shard_map/pallas_call | solution.py:686
